TPU v7x, 256 devices: a whole 4x4x8 slice. The times are simulated.
256 devices in a mesh: tile: 32 (over z_hi, x, core), energy: 8 (over z_lo, y).
Axes of the slice: x: 4, y: 4, z: 8 (z_hi: 4, z_lo: 2; z = z_hi * 2 + z_lo), core: 2. Of those that a mesh axis runs over, the one named last changes fastest.
Arguments:
- object_tiles: float32 [8, 2, 8192, 256], P('energy', None, 'tile'), may hold values from -4 to 4
- probe_field: float32 [8, 2, 128, 128], P('energy'), may hold values from -4 to 4
- intensity: bfloat16 [8, 32, 8, 128, 128], P('energy', 'tile'), may hold values from 0.019897461 to 2
- row_offsets: int32 [32, 8], P('tile'), may hold values from -64 to 192, as said below
- col_offsets: int32 [32, 8], P('tile'), may hold values from 0 to 128
- tile_counts: int32 [32], P('tile'), may hold values from 3 to 8
- material_spectra: float32 [8, 3], replicated, may hold values from 0.2 to 2
Outputs:
- material_maps: float32 [3, 8192, 256], P(None, 'tile')
- model_object: float32 [8, 2, 8192, 256], P('energy', None, 'tile')
Inputs may be any that keep to these rules, and one draw needn't show every extreme that they name: `row_offsets`: in every tile one of slots 0 and 1 starts at -64 and the other at 192.
All inputs are finite; a program needn't handle non-finite values.
Results may differ from a plain program's by a relative error of at most 0.0003.
Values sent between devices are 32-bit elements; how exact they have to be, the bound alone decides.
A program may use at most 64 MiB of HBM per device.

v0:
```python
import math

import jax
import jax.numpy as jnp
from jax import lax
from jax.sharding import PartitionSpec as P

PROBE = 128
NN_ITERS = 8


SMOOTH = 0.01
DAMPING = 0.5


def with_halo(x, sides, width):
    for axis, dim in sides:
        count, length = (lax.axis_size(axis), x.shape[dim])
        up = [(i, (i + 1) % count) for i in range(count - 1)]
        down = [(j, i) for i, j in up]
        last = lax.slice_in_dim(x, length - width, length, axis=dim)
        initial = lax.slice_in_dim(x, 0, width, axis=dim)
        before = lax.ppermute(last, axis, up)
        after = lax.ppermute(initial, axis, down)
        x = jnp.concatenate([before, x, after], axis=dim)
    return x


def from_behind(value, axis, steps):
    count = lax.axis_size(axis)
    initial, last = (max(0, -steps), min(count, count - steps))
    return lax.ppermute(value, axis, [(source, source + steps) for source in range(initial, last)])


def left_apply(table, stack):
    return jnp.einsum(
        "jk,pkl->pjl",
        table,
        stack,
        precision=lax.Precision.HIGHEST,
        preferred_element_type=jnp.float32,
    )


def right_apply(stack, table):
    return jnp.einsum(
        "pjk,kl->pjl",
        stack,
        table,
        precision=lax.Precision.HIGHEST,
        preferred_element_type=jnp.float32,
    )


def tables(length):
    indices = jnp.arange(length, dtype=jnp.int32)
    angles = (
        2.0 * math.pi / length * (indices[:, None] * indices[None, :] % length).astype(jnp.float32)
    )
    return (jnp.cos(angles) / math.sqrt(length), jnp.sin(angles) / math.sqrt(length))


def transform(real_in, imag_in, cos_table, sin_table, direction):
    signed = direction * sin_table
    half_real = left_apply(cos_table, real_in) + left_apply(signed, imag_in)
    half_imag = left_apply(cos_table, imag_in) - left_apply(signed, real_in)
    out_real = right_apply(half_real, cos_table) + right_apply(half_imag, signed)
    out_imag = right_apply(half_imag, cos_table) - right_apply(half_real, signed)
    return (out_real, out_imag)


def unmix_maps(attenuation, spectra):
    step_size = 1.0 / jnp.sum(spectra * spectra)
    materials = jnp.zeros((spectra.shape[1],) + attenuation.shape[1:], attenuation.dtype)
    for iteration in range(NN_ITERS):
        predicted = jnp.sum(spectra[:, :, None, None] * materials[None], axis=1)
        mismatch = predicted - attenuation
        gradient = jnp.sum(spectra[:, :, None, None] * mismatch[:, None], axis=0)
        materials = jnp.maximum(materials - step_size * gradient, 0.0)
    return materials


def body(
    object_tiles, probe_field, intensity, row_offsets, col_offsets, tile_counts, material_spectra
):
    current = object_tiles[0]
    probe_re = probe_field[0, 0]
    probe_im = probe_field[0, 1]
    samples = intensity[0, 0]
    live_count = tile_counts[0]
    width = PROBE
    depth = PROBE // 2
    side = current.shape[1]
    slots = row_offsets.shape[1]
    cos_table, sin_table = tables(width)
    power = probe_re * probe_re + probe_im * probe_im
    row_starts = row_offsets[0] + depth
    col_starts = col_offsets[0]
    active = (jnp.arange(slots, dtype=jnp.int32) < live_count)[:, None, None]
    roots = jnp.sqrt(samples.astype(jnp.float32))
    extended = with_halo(current, (("tile", 1),), depth)

    def cut_window(row_start, col_start):
        anchor = jnp.zeros((), jnp.int32)
        return lax.dynamic_slice(extended, (anchor, row_start, col_start), (2, width, width))

    windows = jax.vmap(cut_window)(row_starts, col_starts)
    exit_re = probe_re * windows[:, 0] - probe_im * windows[:, 1]
    exit_im = probe_re * windows[:, 1] + probe_im * windows[:, 0]
    spec_re, spec_im = transform(exit_re, exit_im, cos_table, sin_table, 1.0)
    factor = roots / jnp.sqrt(spec_re * spec_re + spec_im * spec_im + SMOOTH)
    back_re, back_im = transform(spec_re * factor, spec_im * factor, cos_table, sin_table, -1.0)
    change_re = back_re - exit_re
    change_im = back_im - exit_im
    parts_re = jnp.where(active, probe_re * change_re + probe_im * change_im, 0.0)
    parts_im = jnp.where(active, probe_re * change_im - probe_im * change_re, 0.0)
    placed_power = jnp.where(active, power[None], 0.0)

    def place(position, totals):
        numerator, weights = totals
        row_start = row_starts[position]
        col_start = col_starts[position]
        anchor = jnp.zeros((), jnp.int32)
        parts = jnp.stack([parts_re[position], parts_im[position]])
        previous = lax.dynamic_slice(numerator, (anchor, row_start, col_start), (2, width, width))
        numerator = lax.dynamic_update_slice(
            numerator, previous + parts, (anchor, row_start, col_start)
        )
        older = lax.dynamic_slice(weights, (row_start, col_start), (width, width))
        weights = lax.dynamic_update_slice(
            weights, older + placed_power[position], (row_start, col_start)
        )
        return (numerator, weights)

    init = (jnp.zeros_like(extended), jnp.zeros_like(extended[0]))
    numerator, weights = lax.fori_loop(0, slots, place, init)
    from_above = from_behind((numerator[:, depth + side :], weights[depth + side :]), "tile", 1)
    from_below = from_behind((numerator[:, :depth], weights[:depth]), "tile", -1)
    core_num = numerator[:, depth : depth + side]
    core_weights = weights[depth : depth + side]
    core_num = core_num.at[:, :depth].add(from_above[0]).at[:, side - depth :].add(from_below[0])
    core_weights = core_weights.at[:depth].add(from_above[1]).at[side - depth :].add(from_below[1])
    current = current + core_num / (core_weights + DAMPING)
    squared = current[0] ** 2 + current[1] ** 2 + SMOOTH
    attenuation = -0.5 * jnp.log(squared)
    regrouped = lax.all_to_all(attenuation[None], "energy", split_axis=1, concat_axis=0, tiled=True)
    piece_maps = unmix_maps(regrouped, material_spectra)
    materials = lax.all_gather(piece_maps, "energy", axis=1, tiled=True)
    own_row = lax.dynamic_index_in_dim(
        material_spectra, lax.axis_index("energy"), 0, keepdims=False
    )
    thickness = jnp.sum(own_row[:, None, None] * materials, axis=0)
    scale_out = jnp.exp(-thickness) / jnp.sqrt(squared)
    model_object = (current * scale_out[None])[None]
    return (materials, model_object)


def solution(mesh):
    placed = (
        P("energy", None, "tile", None),
        P("energy", None, None, None),
        P("energy", "tile", None, None, None),
        P("tile", None),
        P("tile", None),
        P("tile"),
        P(),
    )
    return jax.shard_map(
        body,
        mesh=mesh,
        in_specs=placed,
        out_specs=(P(None, "tile", None), P("energy", None, "tile", None)),
        check_vma=False,
    )
```

profile of v0, /device:TPU:71, one launch (start us, length us, event | category | flops | bytes accessed | tf_op | source)
XLA Modules:
  0.0 355.3 jit_solution(117914211898438778)
XLA Ops:
  2.1 6.7 %collective-permute-start = (f32[2,64,256]{2,0,1:T(2,128)S(1)}, f32[2,64,256]{2,0,1:T(2,128)S(1)}, u32[]{:S(2)}, u32[]{:S(2)}) collective-permute-start(f32[2,64,256]{2,0,1:T(2,128)S(1)} %get-tuple-element.250), channel_id=1, source_target_pairs={{0,8},{8,16},{16,24},{24,32},{32,40},{40,48},{48,56},{56,64},{64,7... | collective-permute-start | bytes 393224 | tf_op jit(solution)/shard_map/ppermute | solution.py:23
  8.8 1.9 collective-permute-start.1
  12.8 7.9 %collective-permute-done.1 = f32[2,64,256]{2,0,1:T(2,128)S(1)} collective-permute-done((f32[2,64,256]{2,0,1:T(2,128)S(1)}, f32[2,64,256]{2,0,1:T(2,128)S(1)}, u32[]{:S(2)}, u32[]{:S(2)}) %collective-permute-start.1) | collective-permute-done | bytes 131104 | tf_op jit(solution)/shard_map/ppermute | solution.py:24
  21.1 17.3 %while.21 = (s32[]{:T(128)}, f32[2,384,256]{2,0,1:T(2,128)S(1)}, s32[8,3]{0,1:T(4,128)S(1)}, f32[8,2,128,128]{3,2,0,1:T(8,128)S(1)}, s32[]{:T(128)}) while((s32[]{:T(128)}, f32[2,384,256]{2,0,1:T(2,128)S(1)}, s32[8,3]{0,1:T(4,128)S(1)}, f32[8,2,128,128]{3,2,0,1:T(8,128)S(1)}, s32[]{:T(128)}) %tuple.79), condition=%wide.while_cond.4, body=%wide.while_body.4.sunk | while | flops 2 | bytes 524405 | solution.py:105
  21.8 1.5 constant_dynamic-slice_fusion.12
  23.9 1.5 constant_dynamic-slice_fusion.12
  49.1 1.6 fusion.27
  58.4 232.0 %while.20 = (s32[]{:T(128)}, f32[2,384,256]{2,0,1:T(2,128)S(1)}, f32[384,256]{1,0:T(8,128)S(1)}, s32[8]{0:T(128)S(1)}, s32[8]{0:T(128)S(1)}, /*index=5*/f32[8,12...) while((s32[]{:T(128)}, f32[2,384,256]{2,0,1:T(2,128)S(1)}, ...), condition=%wide.region_3.4_spmd, body=%wide.region_2.3_spmd.sunk | while | flops 81928 | bytes 1769713 | solution.py:136
  63.9 21.6 %dynamic_update_slice.16 = f32[2,384,256]{2,0,1:T(2,128)S(1)} dynamic-update-slice(f32[2,384,256]{2,0,1:T(2,128)S(1)} %get-tuple-element.369, f32[2,128,128]{2,0,1:T(2,128)S(1)} %copy.134, s32[]{:T(128)} %constant.183.clone.1..sunk, s32[]{:T(128)S(6)} %select_n.174, s32[]{:T(128)S(6)} %select_n.175) | dynamic-update-slice | bytes 262148 | tf_op jit(solution)/shard_map/while/body/eval_jaxpr/dynamic_update_slice | solution.py:126
  85.5 1.5 dynamic_update_slice.17
  92.5 21.6 %dynamic_update_slice.16 = f32[2,384,256]{2,0,1:T(2,128)S(1)} dynamic-update-slice(f32[2,384,256]{2,0,1:T(2,128)S(1)} %get-tuple-element.369, f32[2,128,128]{2,0,1:T(2,128)S(1)} %copy.134, s32[]{:T(128)} %constant.183.clone.1..sunk, s32[]{:T(128)S(6)} %select_n.174, s32[]{:T(128)S(6)} %select_n.175) | dynamic-update-slice | bytes 262148 | tf_op jit(solution)/shard_map/while/body/eval_jaxpr/dynamic_update_slice | solution.py:126
  114.2 2.0 dynamic_update_slice.17
  121.7 21.6 %dynamic_update_slice.16 = f32[2,384,256]{2,0,1:T(2,128)S(1)} dynamic-update-slice(f32[2,384,256]{2,0,1:T(2,128)S(1)} %get-tuple-element.369, f32[2,128,128]{2,0,1:T(2,128)S(1)} %copy.134, s32[]{:T(128)} %constant.183.clone.1..sunk, s32[]{:T(128)S(6)} %select_n.174, s32[]{:T(128)S(6)} %select_n.175) | dynamic-update-slice | bytes 262148 | tf_op jit(solution)/shard_map/while/body/eval_jaxpr/dynamic_update_slice | solution.py:126
  143.4 1.8 dynamic_update_slice.17
  150.7 21.6 %dynamic_update_slice.16 = f32[2,384,256]{2,0,1:T(2,128)S(1)} dynamic-update-slice(f32[2,384,256]{2,0,1:T(2,128)S(1)} %get-tuple-element.369, f32[2,128,128]{2,0,1:T(2,128)S(1)} %copy.134, s32[]{:T(128)} %constant.183.clone.1..sunk, s32[]{:T(128)S(6)} %select_n.174, s32[]{:T(128)S(6)} %select_n.175) | dynamic-update-slice | bytes 262148 | tf_op jit(solution)/shard_map/while/body/eval_jaxpr/dynamic_update_slice | solution.py:126
  172.4 2.0 dynamic_update_slice.17
  179.9 21.6 %dynamic_update_slice.16 = f32[2,384,256]{2,0,1:T(2,128)S(1)} dynamic-update-slice(f32[2,384,256]{2,0,1:T(2,128)S(1)} %get-tuple-element.369, f32[2,128,128]{2,0,1:T(2,128)S(1)} %copy.134, s32[]{:T(128)} %constant.183.clone.1..sunk, s32[]{:T(128)S(6)} %select_n.174, s32[]{:T(128)S(6)} %select_n.175) | dynamic-update-slice | bytes 262148 | tf_op jit(solution)/shard_map/while/body/eval_jaxpr/dynamic_update_slice | solution.py:126
  201.6 1.7 dynamic_update_slice.17
  208.8 21.6 %dynamic_update_slice.16 = f32[2,384,256]{2,0,1:T(2,128)S(1)} dynamic-update-slice(f32[2,384,256]{2,0,1:T(2,128)S(1)} %get-tuple-element.369, f32[2,128,128]{2,0,1:T(2,128)S(1)} %copy.134, s32[]{:T(128)} %constant.183.clone.1..sunk, s32[]{:T(128)S(6)} %select_n.174, s32[]{:T(128)S(6)} %select_n.175) | dynamic-update-slice | bytes 262148 | tf_op jit(solution)/shard_map/while/body/eval_jaxpr/dynamic_update_slice | solution.py:126
  230.4 1.9 dynamic_update_slice.17
  237.8 21.6 %dynamic_update_slice.16 = f32[2,384,256]{2,0,1:T(2,128)S(1)} dynamic-update-slice(f32[2,384,256]{2,0,1:T(2,128)S(1)} %get-tuple-element.369, f32[2,128,128]{2,0,1:T(2,128)S(1)} %copy.134, s32[]{:T(128)} %constant.183.clone.1..sunk, s32[]{:T(128)S(6)} %select_n.174, s32[]{:T(128)S(6)} %select_n.175) | dynamic-update-slice | bytes 262148 | tf_op jit(solution)/shard_map/while/body/eval_jaxpr/dynamic_update_slice | solution.py:126
  259.5 1.8 dynamic_update_slice.17
  266.7 21.6 %dynamic_update_slice.16 = f32[2,384,256]{2,0,1:T(2,128)S(1)} dynamic-update-slice(f32[2,384,256]{2,0,1:T(2,128)S(1)} %get-tuple-element.369, f32[2,128,128]{2,0,1:T(2,128)S(1)} %copy.134, s32[]{:T(128)} %constant.183.clone.1..sunk, s32[]{:T(128)S(6)} %select_n.174, s32[]{:T(128)S(6)} %select_n.175) | dynamic-update-slice | bytes 262148 | tf_op jit(solution)/shard_map/while/body/eval_jaxpr/dynamic_update_slice | solution.py:126
  288.4 1.9 dynamic_update_slice.17
  290.4 2.3 collective-permute-start.4
  292.9 2.0 collective-permute-start.5
  295.0 7.8 %collective-permute-start.2 = (f32[2,64,256]{2,0,1:T(2,128)S(1)}, f32[2,64,256]{2,0,1:T(2,128)S(1)}, u32[]{:S(2)}, u32[]{:S(2)}) collective-permute-start(f32[2,64,256]{2,0,1:T(2,128)S(1)} %get-tuple-element.249), channel_id=1, source_target_pairs={{0,8},{8,16},{16,24},{24,32},{32,40},{40,48},{48,56},{56,64},{64,7... | collective-permute-start | bytes 393224 | tf_op jit(solution)/shard_map/ppermute | solution.py:32
  302.7 2.1 collective-permute-start.3
  305.1 9.1 %collective-permute-done.3 = f32[2,64,256]{2,0,1:T(2,128)S(1)} collective-permute-done((f32[2,64,256]{2,0,1:T(2,128)S(1)}, f32[2,64,256]{2,0,1:T(2,128)S(1)}, u32[]{:S(2)}, u32[]{:S(2)}) %collective-permute-start.3) | collective-permute-done | bytes 131104 | tf_op jit(solution)/shard_map/ppermute | solution.py:32
  316.3 4.2 %all-to-all-start = ((f32[1,256,256]{2,0,1:T(1,128)}), f32[1,256,256]{2,0,1:T(1,128)S(1)}, u32[]{:S(2)}, u32[]{:S(2)}) async-start(f32[1,256,256]{2,0,1:T(1,128)} %get-tuple-element.238), calls=%async_computation | async-start | bytes 524288 | tf_op jit(solution)/shard_map/all_to_all | solution.py:146
  322.1 4.5 %all-to-all-done = f32[1,256,256]{2,0,1:T(1,128)S(1)} async-done(((f32[1,256,256]{2,0,1:T(1,128)}), f32[1,256,256]{2,0,1:T(1,128)S(1)}, u32[]{:S(2)}, u32[]{:S(2)}) %all-to-all-start) | async-done | bytes 262176 | tf_op jit(solution)/shard_map/all_to_all | solution.py:146
  329.1 23.7 %all_gather.3 = f32[3,256,256]{2,1,0:T(8,128)S(1)} all-gather(f32[3,32,256]{2,1,0:T(8,128)S(1)} %subtract_maximum_fusion), channel_id=1, replica_groups=mesh['tile'=32,'energy'=8] {'energy'}, dimensions={1}, use_global_device_ids=true | all-gather | bytes 884736 | tf_op jit(solution)/shard_map/all_gather | solution.py:148
  (184 shorter events, 56.6 us)
Async XLA Ops:
  2.1 8.7 %copy-start.2 = (f32[1,2,128,128]{3,2,1,0:T(8,128)S(1)}, f32[1,2,128,128]{3,2,1,0:T(8,128)}, u32[]{:S(2)}) copy-start(f32[1,2,128,128]{3,2,1,0:T(8,128)} %param.18) | copy-start | bytes 393220
  2.1 10.7 %collective-permute-start = (f32[2,64,256]{2,0,1:T(2,128)S(1)}, f32[2,64,256]{2,0,1:T(2,128)S(1)}, u32[]{:S(2)}, u32[]{:S(2)}) collective-permute-start(f32[2,64,256]{2,0,1:T(2,128)S(1)} %get-tuple-element.250), channel_id=1, source_target_pairs={{0,8},{8,16},{16,24},{24,32},{32,40},{40,48},{48,56},{56,64},{64,7... | collective-permute-start | bytes 393224 | tf_op jit(solution)/shard_map/ppermute | solution.py:23
  8.8 11.9 %collective-permute-start.1 = (f32[2,64,256]{2,0,1:T(2,128)S(1)}, f32[2,64,256]{2,0,1:T(2,128)S(1)}, u32[]{:S(2)}, u32[]{:S(2)}) collective-permute-start(f32[2,64,256]{2,0,1:T(2,128)S(1)} %get-tuple-element.251), channel_id=1, source_target_pairs={{8,0},{16,8},{24,16},{32,24},{40,32},{48,40},{56,48},{64,56},{72,6... | collective-permute-start | bytes 393224 | tf_op jit(solution)/shard_map/ppermute | solution.py:24
  10.8 0.7 copy-start.4
  11.5 0.7 copy-start.5
  46.5 1.2 copy-start
  290.4 14.5 %collective-permute-start.4 = (f32[64,256]{1,0:T(8,128)S(1)}, f32[64,256]{1,0:T(8,128)S(1)}, u32[]{:S(2)}, u32[]{:S(2)}) collective-permute-start(f32[64,256]{1,0:T(8,128)S(1)} %get-tuple-element.253), channel_id=1, source_target_pairs={{0,8},{8,16},{16,24},{24,32},{32,40},{40,48},{48,56},{56,64},{64,7... | collective-permute-start | bytes 196616 | tf_op jit(solution)/shard_map/ppermute | solution.py:32
  292.9 12.0 %collective-permute-start.5 = (f32[64,256]{1,0:T(8,128)S(1)}, f32[64,256]{1,0:T(8,128)S(1)}, u32[]{:S(2)}, u32[]{:S(2)}) collective-permute-start(f32[64,256]{1,0:T(8,128)S(1)} %get-tuple-element.252), channel_id=1, source_target_pairs={{8,0},{16,8},{24,16},{32,24},{40,32},{48,40},{56,48},{64,56},{72,6... | collective-permute-start | bytes 196616 | tf_op jit(solution)/shard_map/ppermute | solution.py:32
  295.0 10.0 %collective-permute-start.2 = (f32[2,64,256]{2,0,1:T(2,128)S(1)}, f32[2,64,256]{2,0,1:T(2,128)S(1)}, u32[]{:S(2)}, u32[]{:S(2)}) collective-permute-start(f32[2,64,256]{2,0,1:T(2,128)S(1)} %get-tuple-element.249), channel_id=1, source_target_pairs={{0,8},{8,16},{16,24},{24,32},{32,40},{40,48},{48,56},{56,64},{64,7... | collective-permute-start | bytes 393224 | tf_op jit(solution)/shard_map/ppermute | solution.py:32
  302.7 11.5 %collective-permute-start.3 = (f32[2,64,256]{2,0,1:T(2,128)S(1)}, f32[2,64,256]{2,0,1:T(2,128)S(1)}, u32[]{:S(2)}, u32[]{:S(2)}) collective-permute-start(f32[2,64,256]{2,0,1:T(2,128)S(1)} %get-tuple-element.248), channel_id=1, source_target_pairs={{8,0},{16,8},{24,16},{32,24},{40,32},{48,40},{56,48},{64,56},{72,6... | collective-permute-start | bytes 393224 | tf_op jit(solution)/shard_map/ppermute | solution.py:32
  305.0 9.3 %copy-start.1 = (f32[1,2,256,256]{3,2,1,0:T(8,128)S(1)}, f32[1,2,256,256]{3,2,1,0:T(8,128)}, u32[]{:S(2)}) copy-start(f32[1,2,256,256]{3,2,1,0:T(8,128)} %param.17) | copy-start | bytes 1572868
  315.0 5.5 %copy-start.3 = (f32[8,3]{0,1:T(4,128)S(1)}, f32[8,3]{0,1:T(4,128)}, u32[]{:S(2)}) copy-start(f32[8,3]{0,1:T(4,128)} %param.23) | copy-start | bytes 292
  316.3 10.3 %all-to-all-start = ((f32[1,256,256]{2,0,1:T(1,128)}), f32[1,256,256]{2,0,1:T(1,128)S(1)}, u32[]{:S(2)}, u32[]{:S(2)}) async-start(f32[1,256,256]{2,0,1:T(1,128)} %get-tuple-element.238), calls=%async_computation | async-start | bytes 524288 | tf_op jit(solution)/shard_map/all_to_all | solution.py:146
where the time goes:
time: 359 us; the launch traced here: 355 us
  local copies, waits for them, and re-layouts  222 us (62%)
  loops' own time  31.8 us (9%)
  starting transfers between devices  27 us (8%)
  blocking collectives  23.7 us (7%)
  waiting for transfers between devices  21.6 us (6%)
  matrix products  19.5 us (5%)
  other arithmetic  7.18 us (2%)
    dynamic_update_slice x16, local copies, waits for them, and re-layouts, place(): lax.dynamic_update_slice(numerator, previous + parts, (anchor, row_start,...  173 us
    another operation x1, loops' own time, body(): numerator, weights = lax.fori_loop(0, slots, place, init)  31.6 us
    all_gather x1, blocking collectives, body(): materials = lax.all_gather(piece_maps, 'energy', axis=1, tiled=True)  23.7 us
    gather x32, local copies, waits for them, and re-layouts  17.1 us
    dynamic_update_slice x8, local copies, waits for them, and re-layouts, place(): lax.dynamic_update_slice(weights, older + placed_power[position], (row_st...  14.8 us
    ppermute x4, starting transfers between devices, from_behind(): lax.ppermute(value, axis, [(source, source + steps) for source in range(i...  14.2 us
    dot_general x8, matrix products, left_apply(): jnp.einsum('jk,pkl->pjl', table, stack, precision=lax.Precision.HIGHEST,...  10.3 us
    dot_general x8, matrix products, right_apply(): jnp.einsum('pjk,kl->pjl', stack, table, precision=lax.Precision.HIGHEST,...  9.19 us
  transfers between devices with their start and end apart: 7, of which 3 were waited for; matrix products, arithmetic and copies ran while one was open for 0% of the time, Pallas kernels for 0%

commit v1 on v0

v1 whole, which is shorter than its diff:
```python
import jax
import jax.numpy as jnp
import ml_dtypes
import numpy as np
from jax import lax
from jax.experimental import pallas as pl
from jax.experimental.pallas import tpu as pltpu
from jax.sharding import PartitionSpec as P

PROBE = 128
NN_ITERS = 8
SMOOTH = 0.01
DAMPING = 0.5
SIDE = 256
DEPTH = 64
SLOTS = 8
PAD = 8
ENERGIES = 8
RING = 4
PIECE = 16
MATERIALS = 3

F32 = jnp.float32
BF16 = jnp.bfloat16
MESH = pl.DeviceIdType.MESH


def dft_tables():
    k = np.arange(PROBE)
    angles = 2.0 * np.pi / PROBE * (np.outer(k, k) % PROBE)
    cos, sin = np.cos(angles) / np.sqrt(PROBE), np.sin(angles) / np.sqrt(PROBE)
    table = np.block([[cos, -sin], [sin, cos]])
    out = []
    for full in (table, table.T):
        high = full.astype(np.float32).astype(ml_dtypes.bfloat16)
        low = (full - high.astype(np.float64)).astype(np.float32).astype(ml_dtypes.bfloat16)
        out += [high, low]
    return np.stack(out)


def halves(x):
    high = x.astype(BF16)
    return high, (x - high.astype(F32)).astype(BF16)


def mul(a, b):
    return jnp.dot(a, b, preferred_element_type=F32)


def right_apply(x, high, low):
    xh, xl = halves(x)
    return mul(xh, high) + mul(xl, high) + mul(xh, low)


def left_apply(high, low, x):
    xh, xl = halves(x)
    return mul(high, xh) + mul(high, xl) + mul(low, xh)


def swap_blocks(x):
    n = PROBE
    top = jnp.concatenate([x[:n, :n], x[n:, :n]], axis=1)
    bottom = jnp.concatenate([x[:n, n:], x[n:, n:]], axis=1)
    return jnp.concatenate([top, bottom], axis=0)


def kernel(
    obj, probe, inten, tables, rows, cols, count, spec,
    maps_out, model_out,
    ext, prb, itn, tab, root, part, pw, wsum, wrecv, num, nrecv, unit, att, gath, maps, model,
    load_sem, halo_send, halo_recv, w_send, w_recv, n_send, n_recv, a_send, a_recv, g_send, g_recv, out_sem,
):
    tile = lax.axis_index("tile")
    me = lax.axis_index("energy")
    tiles = lax.axis_size("tile")
    plane, y = me // RING, lax.rem(me, RING)
    has_up, has_dn = tile > 0, tile < tiles - 1
    up, dn = tile - 1, tile + 1

    def peer(d):
        return lax.rem(me + d, ENERGIES)

    barrier = pltpu.get_barrier_semaphore()

    def greet(where):
        pl.semaphore_signal(barrier, inc=1, device_id=where, device_id_type=MESH)

    @pl.when(has_up)
    def _():
        greet((up, me))

    @pl.when(has_dn)
    def _():
        greet((dn, me))

    for d in range(1, ENERGIES):
        greet((tile, peer(d)))

    loads = [
        pltpu.make_async_copy(probe.at[0], prb, load_sem.at[0]),
        pltpu.make_async_copy(inten.at[0, 0], itn, load_sem.at[1]),
        pltpu.make_async_copy(tables, tab, load_sem.at[2]),
    ] + [
        pltpu.make_async_copy(
            obj.at[0, :, :, pl.ds(h * PROBE, PROBE)], ext.at[:, h, pl.ds(DEPTH, SIDE), :], load_sem.at[3 + h]
        )
        for h in range(2)
    ]
    for load in loads:
        load.start()

    greeted = ENERGIES - 1 + has_up.astype(jnp.int32) + has_dn.astype(jnp.int32)
    pl.semaphore_wait(barrier, greeted)

    def remote(src, dst, send, recv, where):
        return pltpu.make_async_remote_copy(
            src_ref=src, dst_ref=dst, send_sem=send, recv_sem=recv, device_id=where, device_id_type=MESH
        )

    def border_pair(src_up, dst_up, src_dn, dst_dn, send, recv, first):
        return (
            remote(src_up, dst_up, send.at[first], recv.at[first], (up, me)),
            remote(src_dn, dst_dn, send.at[first + 1], recv.at[first + 1], (dn, me)),
        )

    def start_borders(pairs):
        @pl.when(has_up)
        def _():
            for to_up, _ in pairs:
                to_up.start()

        @pl.when(has_dn)
        def _():
            for _, to_dn in pairs:
                to_dn.start()

    def wait_borders(pairs):
        @pl.when(has_dn)
        def _():
            for to_up, _ in pairs:
                to_up.wait_recv()

        @pl.when(has_up)
        def _():
            for _, to_dn in pairs:
                to_dn.wait_recv()

    def sent_borders(pairs):
        @pl.when(has_up)
        def _():
            for to_up, _ in pairs:
                to_up.wait_send()

        @pl.when(has_dn)
        def _():
            for _, to_dn in pairs:
                to_dn.wait_send()

    last = SIDE + DEPTH
    halo = [
        border_pair(
            obj.at[0, :, pl.ds(0, DEPTH), pl.ds(h * PROBE, PROBE)],
            ext.at[:, h, pl.ds(last, DEPTH), :],
            obj.at[0, :, pl.ds(SIDE - DEPTH, DEPTH), pl.ds(h * PROBE, PROBE)],
            ext.at[:, h, pl.ds(0, DEPTH), :],
            halo_send, halo_recv, 2 * h,
        )
        for h in range(2)
    ]
    start_borders(halo)

    @pl.when(jnp.logical_not(has_up))
    def _():
        ext[:, :, 0:DEPTH, :] = jnp.zeros((2, 2, DEPTH, PROBE), F32)
        wrecv[0] = jnp.zeros((2, DEPTH, PROBE), F32)
        nrecv[0] = jnp.zeros((2, 2, DEPTH, PROBE), F32)

    @pl.when(jnp.logical_not(has_dn))
    def _():
        ext[:, :, last:, :] = jnp.zeros((2, 2, DEPTH, PROBE), F32)
        wrecv[1] = jnp.zeros((2, DEPTH, PROBE), F32)
        nrecv[1] = jnp.zeros((2, 2, DEPTH, PROBE), F32)

    part[:, :, 0:PAD, :] = jnp.zeros((SLOTS, 2, PAD, PROBE), F32)
    part[:, :, PAD + PROBE :, :] = jnp.zeros((SLOTS, 2, PAD, PROBE), F32)
    pw[:, 0:PAD, :] = jnp.zeros((SLOTS, PAD, PROBE), F32)
    pw[:, PAD + PROBE :, :] = jnp.zeros((SLOTS, PAD, PROBE), F32)

    live = count[0]
    lefts = [cols[0, j] for j in range(SLOTS)]
    tops = [jnp.where(j < live, rows[0, j] + DEPTH, 8 * SIDE) for j in range(SLOTS)]
    lane8 = lax.broadcasted_iota(jnp.int32, (8, PROBE), 1)

    loads[0].wait()
    probe_re, probe_im = prb[0], prb[1]
    power = probe_re * probe_re + probe_im * probe_im
    for j in range(SLOTS):
        pw[j, PAD : PAD + PROBE, :] = pltpu.roll(power, lax.rem(lefts[j], PROBE), 1)

    def placed(read, group, terms):
        left = [jnp.zeros((8, PROBE), F32) for _ in range(terms)]
        right = [jnp.zeros((8, PROBE), F32) for _ in range(terms)]
        for j in range(SLOTS):
            at = jnp.clip(8 * group - tops[j], -PAD, PROBE) + PAD
            inside = lane8 >= lefts[j]
            for c in range(terms):
                value = read(j, c, pl.ds(at, 8))
                left[c] = left[c] + jnp.where(inside, value, 0.0)
                right[c] = right[c] + jnp.where(inside, 0.0, value)
        return left, right

    def place_weights(group, carry):
        left, right = placed(lambda j, c, where: pw[j, where, :], group, 1)
        at = pl.ds(pl.multiple_of(8 * group, 8), 8)
        wsum[0, at, :] = left[0]
        wsum[1, at, :] = right[0]
        return carry

    edge = DEPTH // 8
    whole = (SIDE + 2 * DEPTH) // 8
    lax.fori_loop(0, edge, place_weights, 0)
    lax.fori_loop(whole - edge, whole, place_weights, 0)
    weights = [
        border_pair(
            wsum.at[:, pl.ds(0, DEPTH), :], wrecv.at[1],
            wsum.at[:, pl.ds(last, DEPTH), :], wrecv.at[0],
            w_send, w_recv, 0,
        )
    ]
    start_borders(weights)
    lax.fori_loop(edge, whole - edge, place_weights, 0)

    loads[1].wait()

    def take_roots(pair, carry):
        for s in range(2):
            root[pair, :, s * PROBE : (s + 1) * PROBE] = jnp.sqrt(itn[2 * pair + s].astype(F32))
        return carry

    lax.fori_loop(0, SLOTS // 2, take_roots, 0)

    def coef(e, k):
        return spec[e, k]

    gram = [[None] * MATERIALS for _ in range(MATERIALS)]
    for k in range(MATERIALS):
        for l in range(k, MATERIALS):
            total = coef(0, k) * coef(0, l)
            for e in range(1, ENERGIES):
                total = total + coef(e, k) * coef(e, l)
            gram[k][l] = gram[l][k] = total
    squares = gram[0][0] + gram[1][1] + gram[2][2]

    for load in loads[2:]:
        load.wait()
    wait_borders(halo)

    lane = lax.broadcasted_iota(jnp.int32, (PROBE, PROBE), 1)

    def project(pair, carry):
        exits = []
        for s in range(2):
            j = 2 * pair + s
            top, left = rows[0, j] + DEPTH, cols[0, j]
            turn = lax.rem(PROBE - left, PROBE)
            first = lane < PROBE - left
            view = [
                jnp.where(
                    first,
                    pltpu.roll(ext[c, 0, pl.ds(top, PROBE), :], turn, 1),
                    pltpu.roll(ext[c, 1, pl.ds(top, PROBE), :], turn, 1),
                )
                for c in range(2)
            ]
            pr, pi = prb[0], prb[1]
            exits.append(jnp.concatenate([pr * view[0] - pi * view[1], pr * view[1] + pi * view[0]], axis=1))
        exit_wave = jnp.concatenate(exits, axis=0)
        t_high, t_low, u_high, u_low = tab[0], tab[1], tab[2], tab[3]
        half = swap_blocks(right_apply(exit_wave, t_high, t_low))
        spectrum = left_apply(u_high, u_low, half)
        sr, si = spectrum[:PROBE], spectrum[PROBE:]
        factor = root[pair] * lax.rsqrt(sr * sr + si * si + SMOOTH)
        half = swap_blocks(left_apply(t_high, t_low, jnp.concatenate([sr * factor, si * factor], axis=0)))
        change = right_apply(half, u_high, u_low) - exit_wave
        for s in range(2):
            j = 2 * pair + s
            cr = change[s * PROBE : (s + 1) * PROBE, :PROBE]
            ci = change[s * PROBE : (s + 1) * PROBE, PROBE:]
            pr, pi = prb[0], prb[1]
            turn = lax.rem(cols[0, j], PROBE)
            part[j, 0, PAD : PAD + PROBE, :] = pltpu.roll(pr * cr + pi * ci, turn, 1)
            part[j, 1, PAD : PAD + PROBE, :] = pltpu.roll(pr * ci - pi * cr, turn, 1)
        return carry

    lax.fori_loop(0, SLOTS // 2, project, 0)

    def numerators(group):
        return placed(lambda j, c, where: part[j, c, where, :], group, 2)

    def place_parts(group, carry):
        left, right = numerators(group)
        at = pl.ds(pl.multiple_of(8 * group, 8), 8)
        for c in range(2):
            num[c, 0, at, :] = left[c]
            num[c, 1, at, :] = right[c]
        return carry

    lax.fori_loop(0, edge, place_parts, 0)
    lax.fori_loop(whole - edge, whole, place_parts, 0)
    borders = [
        border_pair(
            num.at[:, :, pl.ds(0, DEPTH), :], nrecv.at[1],
            num.at[:, :, pl.ds(last, DEPTH), :], nrecv.at[0],
            n_send, n_recv, 0,
        )
    ]
    start_borders(borders)

    def renew(group, h, numerator, weight):
        at = pl.ds(pl.multiple_of(8 * group, 8), 8)
        own = pl.ds(pl.multiple_of(8 * group - DEPTH, 8), 8)
        inverse = 1.0 / (weight + DAMPING)
        new = [ext[c, h, at, :] + numerator[c] * inverse for c in range(2)]
        squared = new[0] * new[0] + new[1] * new[1] + SMOOTH
        scale = lax.rsqrt(squared)
        for c in range(2):
            unit[c, own, h * PROBE : (h + 1) * PROBE] = new[c] * scale
        att[own, h * PROBE : (h + 1) * PROBE] = -0.5 * jnp.log(squared)

    def inner_rows(group, carry):
        at = pl.ds(pl.multiple_of(8 * group, 8), 8)
        for h, sums in enumerate(numerators(group)):
            renew(group, h, sums, wsum[h, at, :])
        return carry

    def first_row(f, p):
        fp, fy = f // RING, lax.rem(f, RING)
        start = DEPTH + DEPTH * fp + PIECE * fy if p == 0 else (SIDE - DEPTH) * fp + PIECE * fy
        return pl.multiple_of(start, PIECE)

    def regroup(p):
        return [
            remote(
                att.at[pl.ds(first_row(peer(d), p), PIECE), :], gath.at[p, me],
                a_send.at[p, d - 1], a_recv.at[p, d - 1], (tile, peer(d)),
            )
            for d in range(1, ENERGIES)
        ]

    def send_pixels(p):
        copies = regroup(p)
        for copy in copies:
            copy.start()
        gath[p, me] = att[pl.ds(first_row(me, p), PIECE), :]
        return copies

    lax.fori_loop(2 * edge, whole - 2 * edge, inner_rows, 0)
    to_energies = [send_pixels(0), None]

    lax.fori_loop(edge, 2 * edge, place_parts, 0)
    lax.fori_loop(whole - 2 * edge, whole - edge, place_parts, 0)

    yp = (tile, plane * RING + lax.rem(y + 1, RING))
    ym = (tile, plane * RING + lax.rem(y + RING - 1, RING))
    zz = (tile, (1 - plane) * RING + y)
    far = plane * RING + lax.rem(y + 2, RING)

    def hop(p, route, owner, start, size, where):
        at = pl.ds(pl.multiple_of(first_row(owner, p) + start, 8), size)
        return remote(maps.at[:, at, :], maps.at[:, at, :], g_send.at[p, route], g_recv.at[p, route], where)

    def hops(p):
        return [
            hop(p, 0, me, 0, PIECE, zz),
            hop(p, 1, me, 0, PIECE, yp),
            hop(p, 2, me, 0, PIECE, ym),
            hop(p, 3, zz[1], 0, PIECE, yp),
            hop(p, 4, zz[1], 0, PIECE, ym),
            hop(p, 5, ym[1], 0, PIECE // 2, yp),
            hop(p, 6, yp[1], PIECE // 2, PIECE // 2, ym),
            hop(p, 7, far, 0, PIECE, zz),
        ]

    ways = [hops(0), hops(1)]

    def decompose(p):
        for copy in to_energies[p]:
            copy.wait_recv()
        step = 1.0 / jnp.full((PIECE, SIDE), squares, F32)
        pulls = []
        for k in range(MATERIALS):
            total = coef(0, k) * gath[p, 0]
            for e in range(1, ENERGIES):
                total = total + coef(e, k) * gath[p, e]
            pulls.append(total)
        levels = [jnp.maximum(step * pull, 0.0) for pull in pulls]
        for _ in range(NN_ITERS - 1):
            levels = [
                jnp.maximum(
                    levels[k]
                    - step
                    * (gram[k][0] * levels[0] + gram[k][1] * levels[1] + gram[k][2] * levels[2] - pulls[k]),
                    0.0,
                )
                for k in range(MATERIALS)
            ]
        for k in range(MATERIALS):
            maps[k, pl.ds(first_row(me, p), PIECE), :] = levels[k]
        for way in ways[p][:3]:
            way.start()

    own_spec = [spec[me, k] for k in range(MATERIALS)]
    finished = []

    def finish(owner, p):
        at = pl.ds(first_row(owner, p), PIECE)
        thickness = own_spec[0] * maps[0, at, :] + own_spec[1] * maps[1, at, :] + own_spec[2] * maps[2, at, :]
        fade = jnp.exp(-thickness)
        for c in range(2):
            model[c, at, :] = unit[c, at, :] * fade
        index = 2 * len(finished)
        copies = (
            pltpu.make_async_copy(maps.at[:, at, :], maps_out.at[:, at, :], out_sem.at[index]),
            pltpu.make_async_copy(model.at[:, at, :], model_out.at[0, :, at, :], out_sem.at[index + 1]),
        )
        for copy in copies:
            copy.start()
        finished.append(copies)

    decompose(0)

    wait_borders(weights)
    wait_borders(borders)

    def outer_rows(group, carry):
        for side, base in ((0, edge), (1, whole - 2 * edge)):
            row = pl.ds(pl.multiple_of(8 * group, 8), 8)
            at = pl.ds(pl.multiple_of(8 * (group + base), 8), 8)
            for h in range(2):
                sums = [num[c, h, at, :] + nrecv[side, c, h, row, :] for c in range(2)]
                renew(group + base, h, sums, wsum[h, at, :] + wrecv[side, h, row, :])
        return carry

    lax.fori_loop(0, edge, outer_rows, 0)
    to_energies[1] = send_pixels(1)

    def relay_first(p):
        ways[p][0].wait_recv()
        ways[p][3].start()
        ways[p][4].start()
        ways[p][1].wait_recv()
        ways[p][5].start()
        ways[p][2].wait_recv()
        ways[p][6].start()

    def relay_far(p):
        ways[p][5].wait_recv()
        ways[p][6].wait_recv()
        ways[p][7].start()

    relay_first(0)
    finish(me, 0)
    decompose(1)
    finish(zz[1], 0)
    finish(ym[1], 0)
    finish(yp[1], 0)
    relay_far(0)
    finish(far, 0)
    relay_first(1)
    finish(me, 1)
    finish(zz[1], 1)
    finish(ym[1], 1)
    finish(yp[1], 1)
    relay_far(1)
    finish(far, 1)
    for p in range(2):
        for route, owner in ((3, (1 - plane) * RING + lax.rem(y + RING - 1, RING)), (4, (1 - plane) * RING + lax.rem(y + 1, RING)), (7, (1 - plane) * RING + lax.rem(y + 2, RING))):
            ways[p][route].wait_recv()
            finish(owner, p)

    sent_borders(halo + weights + borders)
    for p in range(2):
        for copy in to_energies[p] + ways[p]:
            copy.wait_send()
    for copies in finished:
        for copy in copies:
            copy.wait()


def body(object_tiles, probe_field, intensity, row_offsets, col_offsets, tile_counts, material_spectra):
    tables = jnp.asarray(dft_tables())
    anywhere = pl.BlockSpec(memory_space=pl.ANY)
    scalars = pl.BlockSpec(memory_space=pltpu.SMEM)
    dma = pltpu.SemaphoreType.DMA
    maps, model = pl.pallas_call(
        kernel,
        out_shape=(
            jax.ShapeDtypeStruct((MATERIALS, SIDE, SIDE), F32),
            jax.ShapeDtypeStruct((1, 2, SIDE, SIDE), F32),
        ),
        in_specs=[anywhere] * 4 + [scalars] * 4,
        out_specs=(anywhere, anywhere),
        scratch_shapes=[
            pltpu.VMEM((2, 2, SIDE + 2 * DEPTH, PROBE), F32),
            pltpu.VMEM((2, PROBE, PROBE), F32),
            pltpu.VMEM((SLOTS, PROBE, PROBE), BF16),
            pltpu.VMEM((4, SIDE, SIDE), BF16),
            pltpu.VMEM((SLOTS // 2, PROBE, SIDE), F32),
            pltpu.VMEM((SLOTS, 2, PROBE + 2 * PAD, PROBE), F32),
            pltpu.VMEM((SLOTS, PROBE + 2 * PAD, PROBE), F32),
            pltpu.VMEM((2, SIDE + 2 * DEPTH, PROBE), F32),
            pltpu.VMEM((2, 2, DEPTH, PROBE), F32),
            pltpu.VMEM((2, 2, SIDE + 2 * DEPTH, PROBE), F32),
            pltpu.VMEM((2, 2, 2, DEPTH, PROBE), F32),
            pltpu.VMEM((2, SIDE, SIDE), F32),
            pltpu.VMEM((SIDE, SIDE), F32),
            pltpu.VMEM((2, ENERGIES, PIECE, SIDE), F32),
            pltpu.VMEM((MATERIALS, SIDE, SIDE), F32),
            pltpu.VMEM((2, SIDE, SIDE), F32),
            dma((5,)),
            dma((4,)), dma((4,)),
            dma((2,)), dma((2,)),
            dma((2,)), dma((2,)),
            dma((2, ENERGIES - 1)), dma((2, ENERGIES - 1)),
            dma((2, 8)), dma((2, 8)),
            dma((4 * ENERGIES,)),
        ],
        compiler_params=pltpu.CompilerParams(collective_id=0, has_side_effects=True),
        name="refine",
    )(object_tiles, probe_field, intensity, tables, row_offsets, col_offsets, tile_counts, material_spectra)
    return (maps, model)


def solution(mesh):
    placed = (
        P("energy", None, "tile", None),
        P("energy", None, None, None),
        P("energy", "tile", None, None, None),
        P("tile", None),
        P("tile", None),
        P("tile"),
        P(),
    )
    return jax.shard_map(
        body,
        mesh=mesh,
        in_specs=placed,
        out_specs=(P(None, "tile", None), P("energy", None, "tile", None)),
        check_vma=False,
    )
```

time: 359 us -> 48.8 us (0.14)
  the two profiles are of different devices: /device:TPU:71 before, /device:TPU:224 now
where the time goes in v1:
time: 48.8 us; the launch traced here: 48.6 us
  Pallas kernels  43.1 us (88%)
  local copies, waits for them, and re-layouts  4.27 us (9%)
  between operations  1.29 us (3%)
    pallas_call x1, Pallas kernels, body(): pl.pallas_call(kernel, out_shape=(jax.ShapeDtypeStruct((MATERIALS, SIDE,...  43.1 us
    unnamed x5, local copies, waits for them, and re-layouts  4.27 us

profile of v1, /device:TPU:224, one launch (start us, length us, event | category | flops | bytes accessed | tf_op | source)
XLA Modules:
  0.0 48.6 jit_solution(408381040839001187)
XLA Ops:
  1.3 1.3 %copy.10.spec = f32[8,3]{1,0:T(8,128)} copy(f32[8,3]{0,1:T(4,128)} %param.14) | data formatting | bytes 192 | tf_op args[6]
  2.6 43.1 %refine.1 = (f32[3,256,256]{2,1,0:T(8,128)}, f32[1,2,256,256]{3,2,1,0:T(8,128)}) custom-call(f32[1,2,256,256]{3,2,1,0:T(8,128)} %obj.1, f32[1,2,128,128]{3,2,1,0:T(8,128)} %probe.1, bf16[1,1,8,128,128]{4,3,2,1,0:T(8,128)(2,1)} %inten.1, bf16[4,256,256]{2,1,0:T(8,128)(2,1)} %constant.2.clone.tables, s32[1,8]{1,0:T(1,128)} %rows.1, s32[1,8]{1,0:T(1,128)} %cols.1, ...), custom_call_target="tpu_custom_call" | custom-call | tf_op jit(solution)/shard_map/refine/pallas_call | solution.py:495
  45.7 0.0 copy-start
  45.7 2.1 %copy.14 = f32[3,256,256]{2,1,0:T(8,128)} copy(f32[3,256,256]{2,1,0:T(8,128)} %get-tuple-element.4) | data formatting | bytes 1572864
  47.8 0.0 copy-done
  47.9 0.8 %copy.15 = f32[1,2,256,256]{3,2,1,0:T(8,128)} copy(f32[1,2,256,256]{3,2,1,0:T(8,128)S(1)} %copy-done) | data formatting | bytes 1048576
Async XLA Ops:
  45.7 2.1 %copy-start = (f32[1,2,256,256]{3,2,1,0:T(8,128)S(1)}, f32[1,2,256,256]{3,2,1,0:T(8,128)}, u32[]{:S(2)}) copy-start(f32[1,2,256,256]{3,2,1,0:T(8,128)} %get-tuple-element.5) | copy-start | bytes 1572868

commit v2 on v1

--- a/solution.py
+++ b/solution.py
@@ -19,6 +19,7 @@
 RING = 4
 PIECE = 16
 MATERIALS = 3
+UNROLL = 4
 
 F32 = jnp.float32
 BF16 = jnp.bfloat16
@@ -65,10 +66,10 @@
 
 
 def kernel(
-    obj, probe, inten, tables, rows, cols, count, spec,
-    maps_out, model_out,
-    ext, prb, itn, tab, root, part, pw, wsum, wrecv, num, nrecv, unit, att, gath, maps, model,
-    load_sem, halo_send, halo_recv, w_send, w_recv, n_send, n_recv, a_send, a_recv, g_send, g_recv, out_sem,
+    obj, probe, inten, tables, rows_in, cols_in, count, spec_in,
+    maps, model,
+    ext, prb, itn, tab, root, part, pw, wsum, wrecv, num, nrecv, unit, att, gath, rows, cols, spec,
+    load_sem, halo_send, halo_recv, w_send, w_recv, n_send, n_recv, a_send, a_recv, g_send, g_recv,
 ):
     tile = lax.axis_index("tile")
     me = lax.axis_index("energy")
@@ -106,7 +107,12 @@
         )
         for h in range(2)
     ]
-    for load in loads:
+    scalars = [
+        pltpu.make_async_copy(rows_in, rows, load_sem.at[5]),
+        pltpu.make_async_copy(cols_in, cols, load_sem.at[6]),
+        pltpu.make_async_copy(spec_in, spec, load_sem.at[7]),
+    ]
+    for load in scalars + loads:
         load.start()
 
     greeted = ENERGIES - 1 + has_up.astype(jnp.int32) + has_dn.astype(jnp.int32)
@@ -186,6 +192,8 @@
     pw[:, 0:PAD, :] = jnp.zeros((SLOTS, PAD, PROBE), F32)
     pw[:, PAD + PROBE :, :] = jnp.zeros((SLOTS, PAD, PROBE), F32)
 
+    for load in scalars:
+        load.wait()
     live = count[0]
     lefts = [cols[0, j] for j in range(SLOTS)]
     tops = [jnp.where(j < live, rows[0, j] + DEPTH, 8 * SIDE) for j in range(SLOTS)]
@@ -240,7 +248,7 @@
     lax.fori_loop(0, SLOTS // 2, take_roots, 0)
 
     def coef(e, k):
-        return spec[e, k]
+        return spec[k, e]
 
     gram = [[None] * MATERIALS for _ in range(MATERIALS)]
     for k in range(MATERIALS):
@@ -292,7 +300,7 @@
             part[j, 1, PAD : PAD + PROBE, :] = pltpu.roll(pr * ci - pi * cr, turn, 1)
         return carry
 
-    lax.fori_loop(0, SLOTS // 2, project, 0)
+    lax.fori_loop(0, SLOTS // 2, project, 0, unroll=UNROLL)
 
     def numerators(group):
         return placed(lambda j, c, where: part[j, c, where, :], group, 2)
@@ -409,26 +417,6 @@
         for way in ways[p][:3]:
             way.start()
 
-    own_spec = [spec[me, k] for k in range(MATERIALS)]
-    finished = []
-
-    def finish(owner, p):
-        at = pl.ds(first_row(owner, p), PIECE)
-        thickness = own_spec[0] * maps[0, at, :] + own_spec[1] * maps[1, at, :] + own_spec[2] * maps[2, at, :]
-        fade = jnp.exp(-thickness)
-        for c in range(2):
-            model[c, at, :] = unit[c, at, :] * fade
-        index = 2 * len(finished)
-        copies = (
-            pltpu.make_async_copy(maps.at[:, at, :], maps_out.at[:, at, :], out_sem.at[index]),
-            pltpu.make_async_copy(model.at[:, at, :], model_out.at[0, :, at, :], out_sem.at[index + 1]),
-        )
-        for copy in copies:
-            copy.start()
-        finished.append(copies)
-
-    decompose(0)
-
     wait_borders(weights)
     wait_borders(borders)
 
@@ -458,48 +446,65 @@
         ways[p][6].wait_recv()
         ways[p][7].start()
 
-    relay_first(0)
-    finish(me, 0)
+    own_spec = [spec[k, me] for k in range(MATERIALS)]
+
+    def finish(owner, p):
+        at = pl.ds(first_row(owner, p), PIECE)
+        thickness = own_spec[0] * maps[0, at, :] + own_spec[1] * maps[1, at, :] + own_spec[2] * maps[2, at, :]
+        fade = jnp.exp(-thickness)
+        for c in range(2):
+            model[c, at, :] = unit[c, at, :] * fade
+
+    decompose(0)
     decompose(1)
-    finish(zz[1], 0)
-    finish(ym[1], 0)
-    finish(yp[1], 0)
-    relay_far(0)
-    finish(far, 0)
-    relay_first(1)
-    finish(me, 1)
-    finish(zz[1], 1)
-    finish(ym[1], 1)
-    finish(yp[1], 1)
-    relay_far(1)
-    finish(far, 1)
     for p in range(2):
-        for route, owner in ((3, (1 - plane) * RING + lax.rem(y + RING - 1, RING)), (4, (1 - plane) * RING + lax.rem(y + 1, RING)), (7, (1 - plane) * RING + lax.rem(y + 2, RING))):
+        finish(me, p)
+    for p in range(2):
+        relay_first(p)
+        for owner in (zz[1], ym[1], yp[1]):
+            finish(owner, p)
+    for p in range(2):
+        relay_far(p)
+        finish(far, p)
+    for p in range(2):
+        for route, owner in ((3, ym), (4, yp), (7, (tile, far))):
             ways[p][route].wait_recv()
-            finish(owner, p)
+            finish(lax.rem(owner[1] + RING, ENERGIES), p)
 
     sent_borders(halo + weights + borders)
     for p in range(2):
         for copy in to_energies[p] + ways[p]:
             copy.wait_send()
-    for copies in finished:
-        for copy in copies:
-            copy.wait()
+
+
+def put_out(maps, model, maps_out, model_out, sems):
+    copies = [
+        pltpu.make_async_copy(maps, maps_out, sems.at[0]),
+        pltpu.make_async_copy(model, model_out.at[0], sems.at[1]),
+    ]
+    for copy in copies:
+        copy.start()
+    for copy in copies:
+        copy.wait()
+
+
+def stay(*arrays):
+    return [pltpu.with_memory_space_constraint(array, pltpu.HBM) for array in arrays]
 
 
 def body(object_tiles, probe_field, intensity, row_offsets, col_offsets, tile_counts, material_spectra):
     tables = jnp.asarray(dft_tables())
     anywhere = pl.BlockSpec(memory_space=pl.ANY)
-    scalars = pl.BlockSpec(memory_space=pltpu.SMEM)
     dma = pltpu.SemaphoreType.DMA
+    vmem = pl.BlockSpec(memory_space=pltpu.VMEM)
     maps, model = pl.pallas_call(
         kernel,
         out_shape=(
             jax.ShapeDtypeStruct((MATERIALS, SIDE, SIDE), F32),
-            jax.ShapeDtypeStruct((1, 2, SIDE, SIDE), F32),
+            jax.ShapeDtypeStruct((2, SIDE, SIDE), F32),
         ),
-        in_specs=[anywhere] * 4 + [scalars] * 4,
-        out_specs=(anywhere, anywhere),
+        in_specs=[anywhere] * 6 + [pl.BlockSpec(memory_space=pltpu.SMEM), anywhere],
+        out_specs=(vmem, vmem),
         scratch_shapes=[
             pltpu.VMEM((2, 2, SIDE + 2 * DEPTH, PROBE), F32),
             pltpu.VMEM((2, PROBE, PROBE), F32),
@@ -515,20 +520,31 @@
             pltpu.VMEM((2, SIDE, SIDE), F32),
             pltpu.VMEM((SIDE, SIDE), F32),
             pltpu.VMEM((2, ENERGIES, PIECE, SIDE), F32),
-            pltpu.VMEM((MATERIALS, SIDE, SIDE), F32),
-            pltpu.VMEM((2, SIDE, SIDE), F32),
-            dma((5,)),
+            pltpu.SMEM((1, SLOTS), jnp.int32),
+            pltpu.SMEM((1, SLOTS), jnp.int32),
+            pltpu.SMEM((MATERIALS, ENERGIES), F32),
+            dma((8,)),
             dma((4,)), dma((4,)),
             dma((2,)), dma((2,)),
             dma((2,)), dma((2,)),
             dma((2, ENERGIES - 1)), dma((2, ENERGIES - 1)),
             dma((2, 8)), dma((2, 8)),
-            dma((4 * ENERGIES,)),
         ],
-        compiler_params=pltpu.CompilerParams(collective_id=0, has_side_effects=True),
+        compiler_params=pltpu.CompilerParams(collective_id=0, has_side_effects=True, vmem_limit_bytes=24 * 2**20),
         name="refine",
-    )(object_tiles, probe_field, intensity, tables, row_offsets, col_offsets, tile_counts, material_spectra)
-    return (maps, model)
+    )(*stay(object_tiles, probe_field, intensity, tables, row_offsets, col_offsets), tile_counts, *stay(material_spectra.T))
+    return pl.pallas_call(
+        put_out,
+        out_shape=(
+            jax.ShapeDtypeStruct((MATERIALS, SIDE, SIDE), F32),
+            jax.ShapeDtypeStruct((1, 2, SIDE, SIDE), F32),
+        ),
+        in_specs=[vmem, vmem],
+        out_specs=(anywhere, anywhere),
+        scratch_shapes=[dma((2,))],
+        compiler_params=pltpu.CompilerParams(vmem_limit_bytes=8 * 2**20),
+        name="put_out",
+    )(maps, model)
 
 
 def solution(mesh):

time: 48.8 us -> 41.6 us (0.85)
  local copies, waits for them, and re-layouts: 4.27 us -> 0 us
  Pallas kernels: 43.1 us -> 40.2 us
    unnamed x5 -> x0, local copies, waits for them, and re-layouts: 4.27 us -> none
    pallas_call x1, Pallas kernels: 43.1 us -> 39.1 us  [body(): pl.pallas_call(kernel, out_shape=(jax.ShapeDtypeStruct((MATERIALS, SIDE,...]
    pallas_call x0 -> x1, Pallas kernels: none -> 1.07 us  [body(): pl.pallas_call(put_out, out_shape=(jax.ShapeDtypeStruct((MATERIALS, SIDE,...]
where the time goes in v2:
time: 41.6 us; the launch traced here: 41.5 us
  Pallas kernels  40.2 us (97%)
  between operations  1.29 us (3%)
    pallas_call x1, Pallas kernels, body(): pl.pallas_call(kernel, out_shape=(jax.ShapeDtypeStruct((MATERIALS, SIDE,...  39.1 us
    pallas_call x1, Pallas kernels, body(): pl.pallas_call(put_out, out_shape=(jax.ShapeDtypeStruct((MATERIALS, SIDE,...  1.07 us

profile of v2, /device:TPU:224, one launch (start us, length us, event | category | flops | bytes accessed | tf_op | source)
XLA Modules:
  0.0 41.5 jit_solution(1332647475243864395)
XLA Ops:
  1.3 39.1 %refine.1 = (f32[3,256,256]{2,1,0:T(8,128)S(1)}, f32[2,256,256]{2,1,0:T(8,128)S(1)}) custom-call(f32[1,2,256,256]{3,2,1,0:T(8,128)} %obj.1, f32[1,2,128,128]{3,2,1,0:T(8,128)} %probe.1, bf16[1,1,8,128,128]{4,3,2,1,0:T(8,128)(2,1)} %inten.1, bf16[4,256,256]{2,1,0:T(8,128)(2,1)} %constant.2.clone.tables, s32[1,8]{1,0:T(1,128)} %rows_in.1, s32[1,8]{1,0:T(1,128)} %cols_in.1, ...), custom_call_target="tpu_custom_call" | custom-call | tf_op jit(solution)/shard_map/refine/pallas_call | solution.py:500
  40.4 1.1 %put_out.1 = (f32[3,256,256]{2,1,0:T(8,128)}, f32[1,2,256,256]{3,2,1,0:T(8,128)}) custom-call(f32[3,256,256]{2,1,0:T(8,128)S(1)} %get-tuple-element.4.maps, f32[2,256,256]{2,1,0:T(8,128)S(1)} %get-tuple-element.5.model), custom_call_target="tpu_custom_call" | custom-call | tf_op jit(solution)/shard_map/put_out/pallas_call | solution.py:536

commit v3 on v2

--- a/solution.py
+++ b/solution.py
@@ -129,8 +129,10 @@
             remote(src_dn, dst_dn, send.at[first + 1], recv.at[first + 1], (dn, me)),
         )
 
+    shares_up = lax.rem(tile, 2) == 1
+
     def start_borders(pairs):
-        @pl.when(has_up)
+        @pl.when(shares_up)
         def _():
             for to_up, _ in pairs:
                 to_up.start()
@@ -139,6 +141,11 @@
         def _():
             for _, to_dn in pairs:
                 to_dn.start()
+
+        @pl.when(jnp.logical_and(has_up, jnp.logical_not(shares_up)))
+        def _():
+            for to_up, _ in pairs:
+                to_up.start()
 
     def wait_borders(pairs):
         @pl.when(has_dn)
@@ -368,25 +375,18 @@
     lax.fori_loop(edge, 2 * edge, place_parts, 0)
     lax.fori_loop(whole - 2 * edge, whole - edge, place_parts, 0)
 
-    yp = (tile, plane * RING + lax.rem(y + 1, RING))
-    ym = (tile, plane * RING + lax.rem(y + RING - 1, RING))
-    zz = (tile, (1 - plane) * RING + y)
-    far = plane * RING + lax.rem(y + 2, RING)
-
-    def hop(p, route, owner, start, size, where):
-        at = pl.ds(pl.multiple_of(first_row(owner, p) + start, 8), size)
-        return remote(maps.at[:, at, :], maps.at[:, at, :], g_send.at[p, route], g_recv.at[p, route], where)
+    def device(planes, steps):
+        return lax.rem(plane + planes, 2) * RING + lax.rem(y + steps + RING, RING)
+
+    steps = ((1, 2), (0, 1), (0, -1), (1, 0), (0, 2), (1, 1), (1, -1))
 
     def hops(p):
+        at = pl.ds(first_row(me, p), PIECE)
         return [
-            hop(p, 0, me, 0, PIECE, zz),
-            hop(p, 1, me, 0, PIECE, yp),
-            hop(p, 2, me, 0, PIECE, ym),
-            hop(p, 3, zz[1], 0, PIECE, yp),
-            hop(p, 4, zz[1], 0, PIECE, ym),
-            hop(p, 5, ym[1], 0, PIECE // 2, yp),
-            hop(p, 6, yp[1], PIECE // 2, PIECE // 2, ym),
-            hop(p, 7, far, 0, PIECE, zz),
+            remote(
+                maps.at[:, at, :], maps.at[:, at, :], g_send.at[p, i], g_recv.at[p, i], (tile, device(planes, step))
+            )
+            for i, (planes, step) in enumerate(steps)
         ]
 
     ways = [hops(0), hops(1)]
@@ -414,7 +414,7 @@
             ]
         for k in range(MATERIALS):
             maps[k, pl.ds(first_row(me, p), PIECE), :] = levels[k]
-        for way in ways[p][:3]:
+        for way in ways[p]:
             way.start()
 
     wait_borders(weights)
@@ -432,20 +432,6 @@
     lax.fori_loop(0, edge, outer_rows, 0)
     to_energies[1] = send_pixels(1)
 
-    def relay_first(p):
-        ways[p][0].wait_recv()
-        ways[p][3].start()
-        ways[p][4].start()
-        ways[p][1].wait_recv()
-        ways[p][5].start()
-        ways[p][2].wait_recv()
-        ways[p][6].start()
-
-    def relay_far(p):
-        ways[p][5].wait_recv()
-        ways[p][6].wait_recv()
-        ways[p][7].start()
-
     own_spec = [spec[k, me] for k in range(MATERIALS)]
 
     def finish(owner, p):
@@ -460,16 +446,9 @@
     for p in range(2):
         finish(me, p)
     for p in range(2):
-        relay_first(p)
-        for owner in (zz[1], ym[1], yp[1]):
-            finish(owner, p)
-    for p in range(2):
-        relay_far(p)
-        finish(far, p)
-    for p in range(2):
-        for route, owner in ((3, ym), (4, yp), (7, (tile, far))):
-            ways[p][route].wait_recv()
-            finish(lax.rem(owner[1] + RING, ENERGIES), p)
+        for i in (1, 2, 3, 4, 5, 6, 0):
+            ways[p][i].wait_recv()
+            finish(device(steps[i][0], -steps[i][1]), p)
 
     sent_borders(halo + weights + borders)
     for p in range(2):
@@ -528,7 +507,7 @@
             dma((2,)), dma((2,)),
             dma((2,)), dma((2,)),
             dma((2, ENERGIES - 1)), dma((2, ENERGIES - 1)),
-            dma((2, 8)), dma((2, 8)),
+            dma((2, ENERGIES - 1)), dma((2, ENERGIES - 1)),
         ],
         compiler_params=pltpu.CompilerParams(collective_id=0, has_side_effects=True, vmem_limit_bytes=24 * 2**20),
         name="refine",

time: 41.6 us -> 37 us (0.89)
  the two profiles are of different devices: /device:TPU:224 before, /device:TPU:71 now
where the time goes in v3:
time: 37 us; the launch traced here: 36.9 us
  Pallas kernels  35.7 us (96%)
  between operations  1.29 us (3%)
    pallas_call x1, Pallas kernels, body(): pl.pallas_call(kernel, out_shape=(jax.ShapeDtypeStruct((MATERIALS, SIDE,...  34.6 us
    pallas_call x1, Pallas kernels, body(): pl.pallas_call(put_out, out_shape=(jax.ShapeDtypeStruct((MATERIALS, SIDE,...  1.07 us

profile of v3, /device:TPU:71, one launch (start us, length us, event | category | flops | bytes accessed | tf_op | source)
XLA Modules:
  0.0 36.9 jit_solution(17058942737651166853)
XLA Ops:
  1.3 34.6 %refine.1 = (f32[3,256,256]{2,1,0:T(8,128)S(1)}, f32[2,256,256]{2,1,0:T(8,128)S(1)}) custom-call(f32[1,2,256,256]{3,2,1,0:T(8,128)} %obj.1, f32[1,2,128,128]{3,2,1,0:T(8,128)} %probe.1, bf16[1,1,8,128,128]{4,3,2,1,0:T(8,128)(2,1)} %inten.1, bf16[4,256,256]{2,1,0:T(8,128)(2,1)} %constant.2.clone.tables, s32[1,8]{1,0:T(1,128)} %rows_in.1, s32[1,8]{1,0:T(1,128)} %cols_in.1, ...), custom_call_target="tpu_custom_call" | custom-call | tf_op jit(solution)/shard_map/refine/pallas_call | solution.py:479
  35.9 1.1 %put_out.1 = (f32[3,256,256]{2,1,0:T(8,128)}, f32[1,2,256,256]{3,2,1,0:T(8,128)}) custom-call(f32[3,256,256]{2,1,0:T(8,128)S(1)} %get-tuple-element.4.maps, f32[2,256,256]{2,1,0:T(8,128)S(1)} %get-tuple-element.5.model), custom_call_target="tpu_custom_call" | custom-call | tf_op jit(solution)/shard_map/put_out/pallas_call | solution.py:515

commit v4 on v3

--- a/solution.py
+++ b/solution.py
@@ -17,9 +17,9 @@
 PAD = 8
 ENERGIES = 8
 RING = 4
-PIECE = 16
+PIECES = (16, 8, 8)
+FAR_FIRST = (6, 2, 5, 3, 7, 1, 4)
 MATERIALS = 3
-UNROLL = 4
 
 F32 = jnp.float32
 BF16 = jnp.bfloat16
@@ -129,45 +129,33 @@
             remote(src_dn, dst_dn, send.at[first + 1], recv.at[first + 1], (dn, me)),
         )
 
-    shares_up = lax.rem(tile, 2) == 1
-
-    def start_borders(pairs):
-        @pl.when(shares_up)
+    odd = lax.rem(tile, 2) == 1
+    even = jnp.logical_not(odd)
+    link_up, link_dn = jnp.logical_and(even, has_up), jnp.logical_and(odd, has_dn)
+    chip_side = 1 - lax.rem(tile, 2)
+    link_side = 1 - chip_side
+
+    def when(condition, action, copies):
+        @pl.when(condition)
         def _():
-            for to_up, _ in pairs:
-                to_up.start()
-
-        @pl.when(has_dn)
-        def _():
-            for _, to_dn in pairs:
-                to_dn.start()
-
-        @pl.when(jnp.logical_and(has_up, jnp.logical_not(shares_up)))
-        def _():
-            for to_up, _ in pairs:
-                to_up.start()
-
-    def wait_borders(pairs):
-        @pl.when(has_dn)
-        def _():
-            for to_up, _ in pairs:
-                to_up.wait_recv()
-
-        @pl.when(has_up)
-        def _():
-            for _, to_dn in pairs:
-                to_dn.wait_recv()
-
-    def sent_borders(pairs):
-        @pl.when(has_up)
-        def _():
-            for to_up, _ in pairs:
-                to_up.wait_send()
-
-        @pl.when(has_dn)
-        def _():
-            for _, to_dn in pairs:
-                to_dn.wait_send()
+            for copy in copies:
+                getattr(copy, action)()
+
+    def start_link(pairs, action="start"):
+        when(link_up, action, [to_up for to_up, _ in pairs])
+        when(link_dn, action, [to_dn for _, to_dn in pairs])
+
+    def start_chip(pairs, action="start"):
+        when(even, action, [to_dn for _, to_dn in pairs])
+        when(odd, action, [to_up for to_up, _ in pairs])
+
+    def wait_link(pairs):
+        when(link_up, "wait_recv", [to_dn for _, to_dn in pairs])
+        when(link_dn, "wait_recv", [to_up for to_up, _ in pairs])
+
+    def wait_chip(pairs):
+        when(even, "wait_recv", [to_up for to_up, _ in pairs])
+        when(odd, "wait_recv", [to_dn for _, to_dn in pairs])
 
     last = SIDE + DEPTH
     halo = [
@@ -180,7 +168,8 @@
         )
         for h in range(2)
     ]
-    start_borders(halo)
+    start_link(halo)
+    start_chip(halo)
 
     @pl.when(jnp.logical_not(has_up))
     def _():
@@ -242,7 +231,8 @@
             w_send, w_recv, 0,
         )
     ]
-    start_borders(weights)
+    start_link(weights)
+    start_chip(weights)
     lax.fori_loop(edge, whole - edge, place_weights, 0)
 
     loads[1].wait()
@@ -268,46 +258,52 @@
 
     for load in loads[2:]:
         load.wait()
-    wait_borders(halo)
+    wait_chip(halo)
+    wait_link(halo)
 
     lane = lax.broadcasted_iota(jnp.int32, (PROBE, PROBE), 1)
 
-    def project(pair, carry):
+    def cut_windows(pair, state):
         exits = []
         for s in range(2):
             j = 2 * pair + s
-            top, left = rows[0, j] + DEPTH, cols[0, j]
-            turn = lax.rem(PROBE - left, PROBE)
-            first = lane < PROBE - left
+            top = pl.ds(rows[0, j] + DEPTH, PROBE)
+            inside = lane >= lefts[j]
+            turn = lax.rem(PROBE - lefts[j], PROBE)
             view = [
-                jnp.where(
-                    first,
-                    pltpu.roll(ext[c, 0, pl.ds(top, PROBE), :], turn, 1),
-                    pltpu.roll(ext[c, 1, pl.ds(top, PROBE), :], turn, 1),
-                )
-                for c in range(2)
+                pltpu.roll(jnp.where(inside, ext[c, 0, top, :], ext[c, 1, top, :]), turn, 1) for c in range(2)
             ]
             pr, pi = prb[0], prb[1]
             exits.append(jnp.concatenate([pr * view[0] - pi * view[1], pr * view[1] + pi * view[0]], axis=1))
-        exit_wave = jnp.concatenate(exits, axis=0)
-        t_high, t_low, u_high, u_low = tab[0], tab[1], tab[2], tab[3]
-        half = swap_blocks(right_apply(exit_wave, t_high, t_low))
-        spectrum = left_apply(u_high, u_low, half)
+        state["exit"] = jnp.concatenate(exits, axis=0)
+
+    def transform_rows(pair, state):
+        state["x"] = swap_blocks(right_apply(state["exit"], tab[0], tab[1]))
+
+    def transform_columns(pair, state):
+        spectrum = left_apply(tab[2], tab[3], state["x"])
         sr, si = spectrum[:PROBE], spectrum[PROBE:]
         factor = root[pair] * lax.rsqrt(sr * sr + si * si + SMOOTH)
-        half = swap_blocks(left_apply(t_high, t_low, jnp.concatenate([sr * factor, si * factor], axis=0)))
-        change = right_apply(half, u_high, u_low) - exit_wave
+        state["x"] = jnp.concatenate([sr * factor, si * factor], axis=0)
+
+    def restore_columns(pair, state):
+        state["x"] = swap_blocks(left_apply(tab[0], tab[1], state["x"]))
+
+    def restore_rows(pair, state):
+        change = right_apply(state["x"], tab[2], tab[3]) - state["exit"]
         for s in range(2):
             j = 2 * pair + s
             cr = change[s * PROBE : (s + 1) * PROBE, :PROBE]
             ci = change[s * PROBE : (s + 1) * PROBE, PROBE:]
             pr, pi = prb[0], prb[1]
-            turn = lax.rem(cols[0, j], PROBE)
+            turn = lax.rem(lefts[j], PROBE)
             part[j, 0, PAD : PAD + PROBE, :] = pltpu.roll(pr * cr + pi * ci, turn, 1)
             part[j, 1, PAD : PAD + PROBE, :] = pltpu.roll(pr * ci - pi * cr, turn, 1)
-        return carry
-
-    lax.fori_loop(0, SLOTS // 2, project, 0, unroll=UNROLL)
+
+    states = [{} for _ in range(SLOTS // 2)]
+    for stage in (cut_windows, transform_rows, transform_columns, restore_columns, restore_rows):
+        for pair in range(SLOTS // 2):
+            stage(pair, states[pair])
 
     def numerators(group):
         return placed(lambda j, c, where: part[j, c, where, :], group, 2)
@@ -320,8 +316,12 @@
             num[c, 1, at, :] = right[c]
         return carry
 
-    lax.fori_loop(0, edge, place_parts, 0)
-    lax.fori_loop(whole - edge, whole, place_parts, 0)
+    def place_edge(side):
+        lax.fori_loop(0, edge, lambda g, carry: place_parts(g + side * (whole - edge), carry), 0)
+
+    def place_next(side):
+        lax.fori_loop(0, edge, lambda g, carry: place_parts(g + edge + side * (whole - 3 * edge), carry), 0)
+
     borders = [
         border_pair(
             num.at[:, :, pl.ds(0, DEPTH), :], nrecv.at[1],
@@ -329,7 +329,10 @@
             n_send, n_recv, 0,
         )
     ]
-    start_borders(borders)
+    place_edge(link_side)
+    start_link(borders)
+    place_edge(chip_side)
+    start_chip(borders)
 
     def renew(group, h, numerator, weight):
         at = pl.ds(pl.multiple_of(8 * group, 8), 8)
@@ -349,57 +352,60 @@
         return carry
 
     def first_row(f, p):
-        fp, fy = f // RING, lax.rem(f, RING)
-        start = DEPTH + DEPTH * fp + PIECE * fy if p == 0 else (SIDE - DEPTH) * fp + PIECE * fy
-        return pl.multiple_of(start, PIECE)
-
-    def regroup(p):
-        return [
+        start = (DEPTH, chip_side * (SIDE - DEPTH), link_side * (SIDE - DEPTH))[p]
+        return pl.multiple_of(start + PIECES[p] * f, 8)
+
+    spots = [sum(PIECES[:p]) for p in range(len(PIECES))]
+
+    def send_pixels(p):
+        spot = pl.ds(spots[p], PIECES[p])
+        copies = [
             remote(
-                att.at[pl.ds(first_row(peer(d), p), PIECE), :], gath.at[p, me],
+                att.at[pl.ds(first_row(peer(d), p), PIECES[p]), :], gath.at[me, spot, :],
                 a_send.at[p, d - 1], a_recv.at[p, d - 1], (tile, peer(d)),
             )
-            for d in range(1, ENERGIES)
+            for d in FAR_FIRST
         ]
-
-    def send_pixels(p):
-        copies = regroup(p)
         for copy in copies:
             copy.start()
-        gath[p, me] = att[pl.ds(first_row(me, p), PIECE), :]
+        gath[me, spot, :] = att[pl.ds(first_row(me, p), PIECES[p]), :]
         return copies
 
     lax.fori_loop(2 * edge, whole - 2 * edge, inner_rows, 0)
-    to_energies = [send_pixels(0), None]
-
-    lax.fori_loop(edge, 2 * edge, place_parts, 0)
-    lax.fori_loop(whole - 2 * edge, whole - edge, place_parts, 0)
+    to_energies = [send_pixels(0)]
+    place_next(chip_side)
 
     def device(planes, steps):
         return lax.rem(plane + planes, 2) * RING + lax.rem(y + steps + RING, RING)
 
-    steps = ((1, 2), (0, 1), (0, -1), (1, 0), (0, 2), (1, 1), (1, -1))
+    def hop(p, i, owner, to):
+        at = pl.ds(first_row(owner, p), PIECES[p])
+        return remote(maps.at[:, at, :], maps.at[:, at, :], g_send.at[p, i], g_recv.at[p, i], (tile, to))
+
+    steps = ((1, 0), (0, 2), (0, 1), (0, -1), (1, 1), (1, -1), (1, 2))
 
     def hops(p):
-        at = pl.ds(first_row(me, p), PIECE)
-        return [
-            remote(
-                maps.at[:, at, :], maps.at[:, at, :], g_send.at[p, i], g_recv.at[p, i], (tile, device(planes, step))
-            )
-            for i, (planes, step) in enumerate(steps)
-        ]
-
-    ways = [hops(0), hops(1)]
+        ways = [hop(p, i, me, device(*step)) for i, step in enumerate(steps)]
+        if p == 0:
+            ways[4:] = [
+                hop(p, 4, device(1, 0), device(0, 1)),
+                hop(p, 5, device(1, 0), device(0, -1)),
+                hop(p, 6, device(0, 2), device(1, 0)),
+            ]
+        return ways
+
+    ways = [hops(p) for p in range(len(PIECES))]
 
     def decompose(p):
         for copy in to_energies[p]:
             copy.wait_recv()
-        step = 1.0 / jnp.full((PIECE, SIDE), squares, F32)
+        spot = pl.ds(spots[p], PIECES[p])
+        step = 1.0 / jnp.full((PIECES[p], SIDE), squares, F32)
         pulls = []
         for k in range(MATERIALS):
-            total = coef(0, k) * gath[p, 0]
+            total = coef(0, k) * gath[0, spot, :]
             for e in range(1, ENERGIES):
-                total = total + coef(e, k) * gath[p, e]
+                total = total + coef(e, k) * gath[e, spot, :]
             pulls.append(total)
         levels = [jnp.maximum(step * pull, 0.0) for pull in pulls]
         for _ in range(NN_ITERS - 1):
@@ -413,47 +419,63 @@
                 for k in range(MATERIALS)
             ]
         for k in range(MATERIALS):
-            maps[k, pl.ds(first_row(me, p), PIECE), :] = levels[k]
-        for way in ways[p]:
-            way.start()
-
-    wait_borders(weights)
-    wait_borders(borders)
-
-    def outer_rows(group, carry):
-        for side, base in ((0, edge), (1, whole - 2 * edge)):
+            maps[k, pl.ds(first_row(me, p), PIECES[p]), :] = levels[k]
+        for i in (0, 1, 2, 3) if p == 0 else (6, 1, 4, 5, 2, 3, 0):
+            ways[p][i].start()
+
+    def outer_rows(side):
+        base = edge + side * (whole - 3 * edge)
+
+        def rows_of(group, carry):
             row = pl.ds(pl.multiple_of(8 * group, 8), 8)
             at = pl.ds(pl.multiple_of(8 * (group + base), 8), 8)
             for h in range(2):
                 sums = [num[c, h, at, :] + nrecv[side, c, h, row, :] for c in range(2)]
                 renew(group + base, h, sums, wsum[h, at, :] + wrecv[side, h, row, :])
-        return carry
-
-    lax.fori_loop(0, edge, outer_rows, 0)
-    to_energies[1] = send_pixels(1)
+            return carry
+
+        lax.fori_loop(0, edge, rows_of, 0)
+
+    wait_chip(weights + borders)
+    outer_rows(chip_side)
+    to_energies.append(send_pixels(1))
+    place_next(link_side)
 
     own_spec = [spec[k, me] for k in range(MATERIALS)]
 
     def finish(owner, p):
-        at = pl.ds(first_row(owner, p), PIECE)
+        at = pl.ds(first_row(owner, p), PIECES[p])
         thickness = own_spec[0] * maps[0, at, :] + own_spec[1] * maps[1, at, :] + own_spec[2] * maps[2, at, :]
         fade = jnp.exp(-thickness)
         for c in range(2):
             model[c, at, :] = unit[c, at, :] * fade
 
     decompose(0)
+    wait_link(weights + borders)
+    outer_rows(link_side)
+    to_energies.append(send_pixels(2))
     decompose(1)
-    for p in range(2):
-        finish(me, p)
-    for p in range(2):
-        for i in (1, 2, 3, 4, 5, 6, 0):
-            ways[p][i].wait_recv()
-            finish(device(steps[i][0], -steps[i][1]), p)
-
-    sent_borders(halo + weights + borders)
-    for p in range(2):
-        for copy in to_energies[p] + ways[p]:
-            copy.wait_send()
+    ways[0][0].wait_recv()
+    ways[0][4].start()
+    ways[0][5].start()
+    ways[0][1].wait_recv()
+    ways[0][6].start()
+    finish(me, 0)
+    finish(me, 1)
+    finish(device(1, 0), 0)
+    finish(device(0, 2), 0)
+    decompose(2)
+    finish(me, 2)
+    for p in range(len(PIECES)):
+        for i, (planes, step) in enumerate(steps):
+            if p > 0 or i > 1:
+                ways[p][i].wait_recv()
+                finish(device(planes, -step), p)
+
+    start_link(halo + weights + borders, "wait_send")
+    start_chip(halo + weights + borders, "wait_send")
+    for copy in sum(to_energies + ways, []):
+        copy.wait_send()
 
 
 def put_out(maps, model, maps_out, model_out, sems):
@@ -498,7 +520,7 @@
             pltpu.VMEM((2, 2, 2, DEPTH, PROBE), F32),
             pltpu.VMEM((2, SIDE, SIDE), F32),
             pltpu.VMEM((SIDE, SIDE), F32),
-            pltpu.VMEM((2, ENERGIES, PIECE, SIDE), F32),
+            pltpu.VMEM((ENERGIES, sum(PIECES), SIDE), F32),
             pltpu.SMEM((1, SLOTS), jnp.int32),
             pltpu.SMEM((1, SLOTS), jnp.int32),
             pltpu.SMEM((MATERIALS, ENERGIES), F32),
@@ -506,8 +528,8 @@
             dma((4,)), dma((4,)),
             dma((2,)), dma((2,)),
             dma((2,)), dma((2,)),
-            dma((2, ENERGIES - 1)), dma((2, ENERGIES - 1)),
-            dma((2, ENERGIES - 1)), dma((2, ENERGIES - 1)),
+            dma((len(PIECES), ENERGIES - 1)), dma((len(PIECES), ENERGIES - 1)),
+            dma((len(PIECES), ENERGIES - 1)), dma((len(PIECES), ENERGIES - 1)),
         ],
         compiler_params=pltpu.CompilerParams(collective_id=0, has_side_effects=True, vmem_limit_bytes=24 * 2**20),
         name="refine",

time: 37 us -> 34.4 us (0.930)
  the two profiles are of different devices: /device:TPU:71 before, /device:TPU:128 now
where the time goes in v4:
time: 34.4 us; the launch traced here: 34.3 us
  Pallas kernels  33.1 us (96%)
  between operations  1.29 us (4%)
    pallas_call x1, Pallas kernels, body(): pl.pallas_call(kernel, out_shape=(jax.ShapeDtypeStruct((MATERIALS, SIDE,...  32 us
    pallas_call x1, Pallas kernels, body(): pl.pallas_call(put_out, out_shape=(jax.ShapeDtypeStruct((MATERIALS, SIDE,...  1.07 us

profile of v4, /device:TPU:128, one launch (start us, length us, event | category | flops | bytes accessed | tf_op | source)
XLA Modules:
  0.0 34.3 jit_solution(14240200684934590166)
XLA Ops:
  1.3 32.0 %refine.1 = (f32[3,256,256]{2,1,0:T(8,128)S(1)}, f32[2,256,256]{2,1,0:T(8,128)S(1)}) custom-call(f32[1,2,256,256]{3,2,1,0:T(8,128)} %obj.1, f32[1,2,128,128]{3,2,1,0:T(8,128)} %probe.1, bf16[1,1,8,128,128]{4,3,2,1,0:T(8,128)(2,1)} %inten.1, bf16[4,256,256]{2,1,0:T(8,128)(2,1)} %constant.2.clone.tables, s32[1,8]{1,0:T(1,128)} %rows_in.1, s32[1,8]{1,0:T(1,128)} %cols_in.1, ...), custom_call_target="tpu_custom_call" | custom-call | tf_op jit(solution)/shard_map/refine/pallas_call | solution.py:501
  33.3 1.1 %put_out.1 = (f32[3,256,256]{2,1,0:T(8,128)}, f32[1,2,256,256]{3,2,1,0:T(8,128)}) custom-call(f32[3,256,256]{2,1,0:T(8,128)S(1)} %get-tuple-element.4.maps, f32[2,256,256]{2,1,0:T(8,128)S(1)} %get-tuple-element.5.model), custom_call_target="tpu_custom_call" | custom-call | tf_op jit(solution)/shard_map/put_out/pallas_call | solution.py:537

commit v5 on v4

--- a/solution.py
+++ b/solution.py
@@ -69,7 +69,7 @@
     obj, probe, inten, tables, rows_in, cols_in, count, spec_in,
     maps, model,
     ext, prb, itn, tab, root, part, pw, wsum, wrecv, num, nrecv, unit, att, gath, rows, cols, spec,
-    load_sem, halo_send, halo_recv, w_send, w_recv, n_send, n_recv, a_send, a_recv, g_send, g_recv,
+    load_sem, b_send, halo_recv, b_recv, a_send, a_recv, g_send, g_recv,
 ):
     tile = lax.axis_index("tile")
     me = lax.axis_index("energy")
@@ -123,11 +123,14 @@
             src_ref=src, dst_ref=dst, send_sem=send, recv_sem=recv, device_id=where, device_id_type=MESH
         )
 
-    def border_pair(src_up, dst_up, src_dn, dst_dn, send, recv, first):
+    def border_pair(src_up, dst_up, src_dn, dst_dn, recv):
         return (
-            remote(src_up, dst_up, send.at[first], recv.at[first], (up, me)),
-            remote(src_dn, dst_dn, send.at[first + 1], recv.at[first + 1], (dn, me)),
+            remote(src_up, dst_up, b_send.at[0], recv.at[0], (up, me)),
+            remote(src_dn, dst_dn, b_send.at[1], recv.at[1], (dn, me)),
         )
+
+    def block_pair(block, recv):
+        return [border_pair(block, block, block, block, recv)]
 
     odd = lax.rem(tile, 2) == 1
     even = jnp.logical_not(odd)
@@ -164,7 +167,7 @@
             ext.at[:, h, pl.ds(last, DEPTH), :],
             obj.at[0, :, pl.ds(SIDE - DEPTH, DEPTH), pl.ds(h * PROBE, PROBE)],
             ext.at[:, h, pl.ds(0, DEPTH), :],
-            halo_send, halo_recv, 2 * h,
+            halo_recv,
         )
         for h in range(2)
     ]
@@ -228,11 +231,9 @@
         border_pair(
             wsum.at[:, pl.ds(0, DEPTH), :], wrecv.at[1],
             wsum.at[:, pl.ds(last, DEPTH), :], wrecv.at[0],
-            w_send, w_recv, 0,
+            b_recv,
         )
     ]
-    start_link(weights)
-    start_chip(weights)
     lax.fori_loop(edge, whole - edge, place_weights, 0)
 
     loads[1].wait()
@@ -258,8 +259,11 @@
 
     for load in loads[2:]:
         load.wait()
-    wait_chip(halo)
-    wait_link(halo)
+    halo_bytes = block_pair(nrecv.at[0], halo_recv)
+    wait_chip(halo_bytes)
+    wait_link(halo_bytes)
+    start_link(weights)
+    start_chip(weights)
 
     lane = lax.broadcasted_iota(jnp.int32, (PROBE, PROBE), 1)
 
@@ -326,7 +330,7 @@
         border_pair(
             num.at[:, :, pl.ds(0, DEPTH), :], nrecv.at[1],
             num.at[:, :, pl.ds(last, DEPTH), :], nrecv.at[0],
-            n_send, n_recv, 0,
+            b_recv,
         )
     ]
     place_edge(link_side)
@@ -359,20 +363,15 @@
 
     def send_pixels(p):
         spot = pl.ds(spots[p], PIECES[p])
-        copies = [
+        for d in FAR_FIRST:
             remote(
                 att.at[pl.ds(first_row(peer(d), p), PIECES[p]), :], gath.at[me, spot, :],
-                a_send.at[p, d - 1], a_recv.at[p, d - 1], (tile, peer(d)),
-            )
-            for d in FAR_FIRST
-        ]
-        for copy in copies:
-            copy.start()
+                a_send.at[0], a_recv.at[p], (tile, peer(d)),
+            ).start()
         gath[me, spot, :] = att[pl.ds(first_row(me, p), PIECES[p]), :]
-        return copies
 
     lax.fori_loop(2 * edge, whole - 2 * edge, inner_rows, 0)
-    to_energies = [send_pixels(0)]
+    send_pixels(0)
     place_next(chip_side)
 
     def device(planes, steps):
@@ -380,25 +379,24 @@
 
     def hop(p, i, owner, to):
         at = pl.ds(first_row(owner, p), PIECES[p])
-        return remote(maps.at[:, at, :], maps.at[:, at, :], g_send.at[p, i], g_recv.at[p, i], (tile, to))
+        return remote(maps.at[:, at, :], maps.at[:, at, :], g_send.at[0], g_recv.at[p + 2 if p > 0 else min(i, 2)], (tile, to))
 
     steps = ((1, 0), (0, 2), (0, 1), (0, -1), (1, 1), (1, -1), (1, 2))
 
     def hops(p):
-        ways = [hop(p, i, me, device(*step)) for i, step in enumerate(steps)]
-        if p == 0:
-            ways[4:] = [
-                hop(p, 4, device(1, 0), device(0, 1)),
-                hop(p, 5, device(1, 0), device(0, -1)),
-                hop(p, 6, device(0, 2), device(1, 0)),
-            ]
-        return ways
+        if p > 0:
+            return [hop(p, i, me, device(*step)) for i, step in enumerate(steps)]
+        return [hop(p, i, me, device(*step)) for i, step in enumerate(steps[:4])] + [
+            hop(p, 4, device(1, 0), device(0, 1)),
+            hop(p, 5, device(1, 0), device(0, -1)),
+            hop(p, 6, device(0, 2), device(1, 0)),
+        ]
 
     ways = [hops(p) for p in range(len(PIECES))]
 
     def decompose(p):
-        for copy in to_energies[p]:
-            copy.wait_recv()
+        block = att.at[pl.ds(0, (ENERGIES - 1) * PIECES[p]), :]
+        remote(block, block, a_send.at[0], a_recv.at[p], (tile, peer(1))).wait_recv()
         spot = pl.ds(spots[p], PIECES[p])
         step = 1.0 / jnp.full((PIECES[p], SIDE), squares, F32)
         pulls = []
@@ -436,46 +434,47 @@
 
         lax.fori_loop(0, edge, rows_of, 0)
 
-    wait_chip(weights + borders)
+    border_bytes = block_pair(num.at[:, :, pl.ds(0, 3 * DEPTH // 2), :], b_recv)
+    wait_chip(border_bytes)
     outer_rows(chip_side)
-    to_energies.append(send_pixels(1))
+    send_pixels(1)
     place_next(link_side)
 
     own_spec = [spec[k, me] for k in range(MATERIALS)]
 
-    def finish(owner, p):
-        at = pl.ds(first_row(owner, p), PIECES[p])
+    def finish(p):
+        at = pl.ds(first_row(0, p), ENERGIES * PIECES[p])
         thickness = own_spec[0] * maps[0, at, :] + own_spec[1] * maps[1, at, :] + own_spec[2] * maps[2, at, :]
         fade = jnp.exp(-thickness)
         for c in range(2):
             model[c, at, :] = unit[c, at, :] * fade
 
+    def arrived(p, pieces):
+        block = maps.at[:, pl.ds(0, pieces * PIECES[p]), :]
+        remote(block, block, g_send.at[0], g_recv.at[p + 2], (tile, peer(1))).wait_recv()
+
+    wait_link(border_bytes)
+    outer_rows(link_side)
+    send_pixels(2)
     decompose(0)
-    wait_link(weights + borders)
-    outer_rows(link_side)
-    to_energies.append(send_pixels(2))
     decompose(1)
     ways[0][0].wait_recv()
     ways[0][4].start()
     ways[0][5].start()
     ways[0][1].wait_recv()
     ways[0][6].start()
-    finish(me, 0)
-    finish(me, 1)
-    finish(device(1, 0), 0)
-    finish(device(0, 2), 0)
     decompose(2)
-    finish(me, 2)
     for p in range(len(PIECES)):
-        for i, (planes, step) in enumerate(steps):
-            if p > 0 or i > 1:
-                ways[p][i].wait_recv()
-                finish(device(planes, -step), p)
-
-    start_link(halo + weights + borders, "wait_send")
-    start_chip(halo + weights + borders, "wait_send")
-    for copy in sum(to_energies + ways, []):
-        copy.wait_send()
+        arrived(p, ENERGIES - 3 if p == 0 else ENERGIES - 1)
+        finish(p)
+
+    sent_bytes = block_pair(num.at[:, :, pl.ds(0, 5 * DEPTH // 2), :], b_recv)
+    start_link(sent_bytes, "wait_send")
+    start_chip(sent_bytes, "wait_send")
+    block = att.at[pl.ds(0, (ENERGIES - 1) * sum(PIECES)), :]
+    remote(block, block, a_send.at[0], a_recv.at[0], (tile, peer(1))).wait_send()
+    block = maps.at[:, pl.ds(0, (ENERGIES - 1) * sum(PIECES)), :]
+    remote(block, block, g_send.at[0], g_recv.at[0], (tile, peer(1))).wait_send()
 
 
 def put_out(maps, model, maps_out, model_out, sems):
@@ -524,12 +523,7 @@
             pltpu.SMEM((1, SLOTS), jnp.int32),
             pltpu.SMEM((1, SLOTS), jnp.int32),
             pltpu.SMEM((MATERIALS, ENERGIES), F32),
-            dma((8,)),
-            dma((4,)), dma((4,)),
-            dma((2,)), dma((2,)),
-            dma((2,)), dma((2,)),
-            dma((len(PIECES), ENERGIES - 1)), dma((len(PIECES), ENERGIES - 1)),
-            dma((len(PIECES), ENERGIES - 1)), dma((len(PIECES), ENERGIES - 1)),
+            dma((8,)), dma((2,)), dma((2,)), dma((2,)), dma((1,)), dma((len(PIECES),)), dma((1,)), dma((len(PIECES) + 2,)),
         ],
         compiler_params=pltpu.CompilerParams(collective_id=0, has_side_effects=True, vmem_limit_bytes=24 * 2**20),
         name="refine",

time: 34.4 us -> 33.7 us (0.980)
  the two profiles are of different devices: /device:TPU:128 before, /device:TPU:71 now
where the time goes in v5:
time: 33.7 us; the launch traced here: 33.6 us
  Pallas kernels  32.3 us (96%)
  between operations  1.29 us (4%)
    pallas_call x1, Pallas kernels, body(): pl.pallas_call(kernel, out_shape=(jax.ShapeDtypeStruct((MATERIALS, SIDE,...  31.3 us
    pallas_call x1, Pallas kernels, body(): pl.pallas_call(put_out, out_shape=(jax.ShapeDtypeStruct((MATERIALS, SIDE,...  1.07 us

profile of v5, /device:TPU:71, one launch (start us, length us, event | category | flops | bytes accessed | tf_op | source)
XLA Modules:
  0.0 33.6 jit_solution(17037328143142710837)
XLA Ops:
  1.3 31.3 %refine.1 = (f32[3,256,256]{2,1,0:T(8,128)S(1)}, f32[2,256,256]{2,1,0:T(8,128)S(1)}) custom-call(f32[1,2,256,256]{3,2,1,0:T(8,128)} %obj.1, f32[1,2,128,128]{3,2,1,0:T(8,128)} %probe.1, bf16[1,1,8,128,128]{4,3,2,1,0:T(8,128)(2,1)} %inten.1, bf16[4,256,256]{2,1,0:T(8,128)(2,1)} %constant.2.clone.tables, s32[1,8]{1,0:T(1,128)} %rows_in.1, s32[1,8]{1,0:T(1,128)} %cols_in.1, ...), custom_call_target="tpu_custom_call" | custom-call | tf_op jit(solution)/shard_map/refine/pallas_call | solution.py:500
  32.6 1.1 %put_out.1 = (f32[3,256,256]{2,1,0:T(8,128)}, f32[1,2,256,256]{3,2,1,0:T(8,128)}) custom-call(f32[3,256,256]{2,1,0:T(8,128)S(1)} %get-tuple-element.4.maps, f32[2,256,256]{2,1,0:T(8,128)S(1)} %get-tuple-element.5.model), custom_call_target="tpu_custom_call" | custom-call | tf_op jit(solution)/shard_map/put_out/pallas_call | solution.py:531

commit v6 on v5

--- a/solution.py
+++ b/solution.py
@@ -461,9 +461,9 @@
     ways[0][0].wait_recv()
     ways[0][4].start()
     ways[0][5].start()
+    decompose(2)
     ways[0][1].wait_recv()
     ways[0][6].start()
-    decompose(2)
     for p in range(len(PIECES)):
         arrived(p, ENERGIES - 3 if p == 0 else ENERGIES - 1)
         finish(p)

time: 33.7 us -> 32.4 us (0.961)
  Pallas kernels: 32.3 us -> 31.1 us
    pallas_call x1, Pallas kernels: 31.3 us -> 30 us  [body(): pl.pallas_call(kernel, out_shape=(jax.ShapeDtypeStruct((MATERIALS, SIDE,...]
where the time goes in v6:
time: 32.4 us
  Pallas kernels  31.1 us (96%)
  between operations  1.29 us (4%)
    pallas_call x1, Pallas kernels, body(): pl.pallas_call(kernel, out_shape=(jax.ShapeDtypeStruct((MATERIALS, SIDE,...  30 us
    pallas_call x1, Pallas kernels, body(): pl.pallas_call(put_out, out_shape=(jax.ShapeDtypeStruct((MATERIALS, SIDE,...  1.07 us

profile of v6, /device:TPU:71, one launch (start us, length us, event | category | flops | bytes accessed | tf_op | source)
XLA Modules:
  0.0 32.4 jit_solution(7513160294849990982)
XLA Ops:
  1.3 30.0 %refine.1 = (f32[3,256,256]{2,1,0:T(8,128)S(1)}, f32[2,256,256]{2,1,0:T(8,128)S(1)}) custom-call(f32[1,2,256,256]{3,2,1,0:T(8,128)} %obj.1, f32[1,2,128,128]{3,2,1,0:T(8,128)} %probe.1, bf16[1,1,8,128,128]{4,3,2,1,0:T(8,128)(2,1)} %inten.1, bf16[4,256,256]{2,1,0:T(8,128)(2,1)} %constant.2.clone.tables, s32[1,8]{1,0:T(1,128)} %rows_in.1, s32[1,8]{1,0:T(1,128)} %cols_in.1, ...), custom_call_target="tpu_custom_call" | custom-call | tf_op jit(solution)/shard_map/refine/pallas_call | solution.py:500
  31.3 1.1 %put_out.1 = (f32[3,256,256]{2,1,0:T(8,128)}, f32[1,2,256,256]{3,2,1,0:T(8,128)}) custom-call(f32[3,256,256]{2,1,0:T(8,128)S(1)} %get-tuple-element.4.maps, f32[2,256,256]{2,1,0:T(8,128)S(1)} %get-tuple-element.5.model), custom_call_target="tpu_custom_call" | custom-call | tf_op jit(solution)/shard_map/put_out/pallas_call | solution.py:531

commit v7 on v6

--- a/solution.py
+++ b/solution.py
@@ -98,21 +98,21 @@
         greet((tile, peer(d)))
 
     loads = [
-        pltpu.make_async_copy(probe.at[0], prb, load_sem.at[0]),
-        pltpu.make_async_copy(inten.at[0, 0], itn, load_sem.at[1]),
-        pltpu.make_async_copy(tables, tab, load_sem.at[2]),
-    ] + [
         pltpu.make_async_copy(
-            obj.at[0, :, :, pl.ds(h * PROBE, PROBE)], ext.at[:, h, pl.ds(DEPTH, SIDE), :], load_sem.at[3 + h]
+            obj.at[0, :, :, pl.ds(h * PROBE, PROBE)], ext.at[:, h, pl.ds(DEPTH, SIDE), :], load_sem.at[h]
         )
         for h in range(2)
+    ] + [
+        pltpu.make_async_copy(probe.at[0], prb, load_sem.at[2]),
+        pltpu.make_async_copy(inten.at[0, 0], itn, load_sem.at[3]),
+        pltpu.make_async_copy(tables, tab, load_sem.at[4]),
     ]
     scalars = [
         pltpu.make_async_copy(rows_in, rows, load_sem.at[5]),
         pltpu.make_async_copy(cols_in, cols, load_sem.at[6]),
         pltpu.make_async_copy(spec_in, spec, load_sem.at[7]),
     ]
-    for load in scalars + loads:
+    for load in loads[:2] + scalars + loads[2:]:
         load.start()
 
     greeted = ENERGIES - 1 + has_up.astype(jnp.int32) + has_dn.astype(jnp.int32)
@@ -161,15 +161,14 @@
         when(odd, "wait_recv", [to_dn for _, to_dn in pairs])
 
     last = SIDE + DEPTH
+    for load in loads[:2]:
+        load.wait()
     halo = [
         border_pair(
-            obj.at[0, :, pl.ds(0, DEPTH), pl.ds(h * PROBE, PROBE)],
-            ext.at[:, h, pl.ds(last, DEPTH), :],
-            obj.at[0, :, pl.ds(SIDE - DEPTH, DEPTH), pl.ds(h * PROBE, PROBE)],
-            ext.at[:, h, pl.ds(0, DEPTH), :],
+            ext.at[:, :, pl.ds(DEPTH, DEPTH), :], ext.at[:, :, pl.ds(last, DEPTH), :],
+            ext.at[:, :, pl.ds(SIDE, DEPTH), :], ext.at[:, :, pl.ds(0, DEPTH), :],
             halo_recv,
         )
-        for h in range(2)
     ]
     start_link(halo)
     start_chip(halo)
@@ -198,7 +197,7 @@
     tops = [jnp.where(j < live, rows[0, j] + DEPTH, 8 * SIDE) for j in range(SLOTS)]
     lane8 = lax.broadcasted_iota(jnp.int32, (8, PROBE), 1)
 
-    loads[0].wait()
+    loads[2].wait()
     probe_re, probe_im = prb[0], prb[1]
     power = probe_re * probe_re + probe_im * probe_im
     for j in range(SLOTS):
@@ -236,7 +235,7 @@
     ]
     lax.fori_loop(edge, whole - edge, place_weights, 0)
 
-    loads[1].wait()
+    loads[3].wait()
 
     def take_roots(pair, carry):
         for s in range(2):
@@ -257,11 +256,9 @@
             gram[k][l] = gram[l][k] = total
     squares = gram[0][0] + gram[1][1] + gram[2][2]
 
-    for load in loads[2:]:
-        load.wait()
-    halo_bytes = block_pair(nrecv.at[0], halo_recv)
-    wait_chip(halo_bytes)
-    wait_link(halo_bytes)
+    loads[4].wait()
+    wait_chip(halo)
+    wait_link(halo)
     start_link(weights)
     start_chip(weights)
 

time: 32.4 us -> 32.2 us (level)
  no operation moved by 1% of the time
where the time goes in v7:
time: 32.2 us; the launch traced here: 32.1 us
  Pallas kernels  30.8 us (96%)
  between operations  1.29 us (4%)
    pallas_call x1, Pallas kernels, body(): pl.pallas_call(kernel, out_shape=(jax.ShapeDtypeStruct((MATERIALS, SIDE,...  29.8 us
    pallas_call x1, Pallas kernels, body(): pl.pallas_call(put_out, out_shape=(jax.ShapeDtypeStruct((MATERIALS, SIDE,...  1.07 us

profile of v7, /device:TPU:71, one launch (start us, length us, event | category | flops | bytes accessed | tf_op | source)
XLA Modules:
  0.0 32.1 jit_solution(1863897467913458024)
XLA Ops:
  1.3 29.8 %refine.1 = (f32[3,256,256]{2,1,0:T(8,128)S(1)}, f32[2,256,256]{2,1,0:T(8,128)S(1)}) custom-call(f32[1,2,256,256]{3,2,1,0:T(8,128)} %obj.1, f32[1,2,128,128]{3,2,1,0:T(8,128)} %probe.1, bf16[1,1,8,128,128]{4,3,2,1,0:T(8,128)(2,1)} %inten.1, bf16[4,256,256]{2,1,0:T(8,128)(2,1)} %constant.2.clone.tables, s32[1,8]{1,0:T(1,128)} %rows_in.1, s32[1,8]{1,0:T(1,128)} %cols_in.1, ...), custom_call_target="tpu_custom_call" | custom-call | tf_op jit(solution)/shard_map/refine/pallas_call | solution.py:497
  31.0 1.1 %put_out.1 = (f32[3,256,256]{2,1,0:T(8,128)}, f32[1,2,256,256]{3,2,1,0:T(8,128)}) custom-call(f32[3,256,256]{2,1,0:T(8,128)S(1)} %get-tuple-element.4.maps, f32[2,256,256]{2,1,0:T(8,128)S(1)} %get-tuple-element.5.model), custom_call_target="tpu_custom_call" | custom-call | tf_op jit(solution)/shard_map/put_out/pallas_call | solution.py:528

commit v8 on v7

--- a/solution.py
+++ b/solution.py
@@ -224,8 +224,8 @@
 
     edge = DEPTH // 8
     whole = (SIDE + 2 * DEPTH) // 8
-    lax.fori_loop(0, edge, place_weights, 0)
-    lax.fori_loop(whole - edge, whole, place_weights, 0)
+    lax.fori_loop(0, edge, place_weights, 0, unroll=4)
+    lax.fori_loop(whole - edge, whole, place_weights, 0, unroll=4)
     weights = [
         border_pair(
             wsum.at[:, pl.ds(0, DEPTH), :], wrecv.at[1],
@@ -233,7 +233,7 @@
             b_recv,
         )
     ]
-    lax.fori_loop(edge, whole - edge, place_weights, 0)
+    lax.fori_loop(edge, whole - edge, place_weights, 0, unroll=4)
 
     loads[3].wait()
 
@@ -318,10 +318,10 @@
         return carry
 
     def place_edge(side):
-        lax.fori_loop(0, edge, lambda g, carry: place_parts(g + side * (whole - edge), carry), 0)
+        lax.fori_loop(0, edge, lambda g, carry: place_parts(g + side * (whole - edge), carry), 0, unroll=8)
 
     def place_next(side):
-        lax.fori_loop(0, edge, lambda g, carry: place_parts(g + edge + side * (whole - 3 * edge), carry), 0)
+        lax.fori_loop(0, edge, lambda g, carry: place_parts(g + edge + side * (whole - 3 * edge), carry), 0, unroll=8)
 
     borders = [
         border_pair(
@@ -367,7 +367,7 @@
             ).start()
         gath[me, spot, :] = att[pl.ds(first_row(me, p), PIECES[p]), :]
 
-    lax.fori_loop(2 * edge, whole - 2 * edge, inner_rows, 0)
+    lax.fori_loop(2 * edge, whole - 2 * edge, inner_rows, 0, unroll=8)
     send_pixels(0)
     place_next(chip_side)
 
@@ -429,7 +429,7 @@
                 renew(group + base, h, sums, wsum[h, at, :] + wrecv[side, h, row, :])
             return carry
 
-        lax.fori_loop(0, edge, rows_of, 0)
+        lax.fori_loop(0, edge, rows_of, 0, unroll=8)
 
     border_bytes = block_pair(num.at[:, :, pl.ds(0, 3 * DEPTH // 2), :], b_recv)
     wait_chip(border_bytes)

time: 32.2 us -> 32 us (level)
  no operation moved by 1% of the time
where the time goes in v8:
time: 32 us
  Pallas kernels  30.7 us (96%)
  between operations  1.29 us (4%)
    pallas_call x1, Pallas kernels, body(): pl.pallas_call(kernel, out_shape=(jax.ShapeDtypeStruct((MATERIALS, SIDE,...  29.6 us
    pallas_call x1, Pallas kernels, body(): pl.pallas_call(put_out, out_shape=(jax.ShapeDtypeStruct((MATERIALS, SIDE,...  1.07 us

profile of v8, /device:TPU:71, one launch (start us, length us, event | category | flops | bytes accessed | tf_op | source)
XLA Modules:
  0.0 32.0 jit_solution(7643636769650169377)
XLA Ops:
  1.3 29.6 %refine.1 = (f32[3,256,256]{2,1,0:T(8,128)S(1)}, f32[2,256,256]{2,1,0:T(8,128)S(1)}) custom-call(f32[1,2,256,256]{3,2,1,0:T(8,128)} %obj.1, f32[1,2,128,128]{3,2,1,0:T(8,128)} %probe.1, bf16[1,1,8,128,128]{4,3,2,1,0:T(8,128)(2,1)} %inten.1, bf16[4,256,256]{2,1,0:T(8,128)(2,1)} %constant.2.clone.tables, s32[1,8]{1,0:T(1,128)} %rows_in.1, s32[1,8]{1,0:T(1,128)} %cols_in.1, ...), custom_call_target="tpu_custom_call" | custom-call | tf_op jit(solution)/shard_map/refine/pallas_call | solution.py:497
  30.9 1.1 %put_out.1 = (f32[3,256,256]{2,1,0:T(8,128)}, f32[1,2,256,256]{3,2,1,0:T(8,128)}) custom-call(f32[3,256,256]{2,1,0:T(8,128)S(1)} %get-tuple-element.4.maps, f32[2,256,256]{2,1,0:T(8,128)S(1)} %get-tuple-element.5.model), custom_call_target="tpu_custom_call" | custom-call | tf_op jit(solution)/shard_map/put_out/pallas_call | solution.py:528

commit v9 on v8

--- a/solution.py
+++ b/solution.py
@@ -76,7 +76,7 @@
     tiles = lax.axis_size("tile")
     plane, y = me // RING, lax.rem(me, RING)
     has_up, has_dn = tile > 0, tile < tiles - 1
-    up, dn = tile - 1, tile + 1
+    up, dn = lax.rem(tile + tiles - 1, tiles), lax.rem(tile + 1, tiles)
 
     def peer(d):
         return lax.rem(me + d, ENERGIES)
@@ -415,7 +415,7 @@
             ]
         for k in range(MATERIALS):
             maps[k, pl.ds(first_row(me, p), PIECES[p]), :] = levels[k]
-        for i in (0, 1, 2, 3) if p == 0 else (6, 1, 4, 5, 2, 3, 0):
+        for i in (1, 0, 2, 3) if p == 0 else (6, 1, 4, 5, 2, 3, 0):
             ways[p][i].start()
 
     def outer_rows(side):

time: 32 us -> 32 us (level)
  no operation moved by 1% of the time
where the time goes in v9:
time: 32 us
  Pallas kernels  30.7 us (96%)
  between operations  1.29 us (4%)
    pallas_call x1, Pallas kernels, body(): pl.pallas_call(kernel, out_shape=(jax.ShapeDtypeStruct((MATERIALS, SIDE,...  29.6 us
    pallas_call x1, Pallas kernels, body(): pl.pallas_call(put_out, out_shape=(jax.ShapeDtypeStruct((MATERIALS, SIDE,...  1.07 us

profile of v9, /device:TPU:71, one launch (start us, length us, event | category | flops | bytes accessed | tf_op | source)
XLA Modules:
  0.0 32.0 jit_solution(3068768937666970998)
XLA Ops:
  1.3 29.6 %refine.1 = (f32[3,256,256]{2,1,0:T(8,128)S(1)}, f32[2,256,256]{2,1,0:T(8,128)S(1)}) custom-call(f32[1,2,256,256]{3,2,1,0:T(8,128)} %obj.1, f32[1,2,128,128]{3,2,1,0:T(8,128)} %probe.1, bf16[1,1,8,128,128]{4,3,2,1,0:T(8,128)(2,1)} %inten.1, bf16[4,256,256]{2,1,0:T(8,128)(2,1)} %constant.2.clone.tables, s32[1,8]{1,0:T(1,128)} %rows_in.1, s32[1,8]{1,0:T(1,128)} %cols_in.1, ...), custom_call_target="tpu_custom_call" | custom-call | tf_op jit(solution)/shard_map/refine/pallas_call | solution.py:497
  30.9 1.1 %put_out.1 = (f32[3,256,256]{2,1,0:T(8,128)}, f32[1,2,256,256]{3,2,1,0:T(8,128)}) custom-call(f32[3,256,256]{2,1,0:T(8,128)S(1)} %get-tuple-element.4.maps, f32[2,256,256]{2,1,0:T(8,128)S(1)} %get-tuple-element.5.model), custom_call_target="tpu_custom_call" | custom-call | tf_op jit(solution)/shard_map/put_out/pallas_call | solution.py:528

commit v10 on v9

--- a/solution.py
+++ b/solution.py
@@ -402,14 +402,13 @@
             for e in range(1, ENERGIES):
                 total = total + coef(e, k) * gath[e, spot, :]
             pulls.append(total)
-        levels = [jnp.maximum(step * pull, 0.0) for pull in pulls]
+        keep = [[(1.0 if k == l else 0.0) - step * gram[k][l] for l in range(MATERIALS)] for k in range(MATERIALS)]
+        gains = [step * pull for pull in pulls]
+        levels = [jnp.maximum(gain, 0.0) for gain in gains]
         for _ in range(NN_ITERS - 1):
             levels = [
                 jnp.maximum(
-                    levels[k]
-                    - step
-                    * (gram[k][0] * levels[0] + gram[k][1] * levels[1] + gram[k][2] * levels[2] - pulls[k]),
-                    0.0,
+                    (keep[k][0] * levels[0] + keep[k][1] * levels[1]) + (keep[k][2] * levels[2] + gains[k]), 0.0
                 )
                 for k in range(MATERIALS)
             ]

time: 32 us -> 32.1 us (level)
  no operation moved by 1% of the time
where the time goes in v10:
time: 32.1 us; the launch traced here: 32 us
  Pallas kernels  30.7 us (96%)
  between operations  1.29 us (4%)
    pallas_call x1, Pallas kernels, body(): pl.pallas_call(kernel, out_shape=(jax.ShapeDtypeStruct((MATERIALS, SIDE,...  29.6 us
    pallas_call x1, Pallas kernels, body(): pl.pallas_call(put_out, out_shape=(jax.ShapeDtypeStruct((MATERIALS, SIDE,...  1.07 us

profile of v10, /device:TPU:71, one launch (start us, length us, event | category | flops | bytes accessed | tf_op | source)
XLA Modules:
  0.0 32.0 jit_solution(3318642552899672749)
XLA Ops:
  1.3 29.6 %refine.1 = (f32[3,256,256]{2,1,0:T(8,128)S(1)}, f32[2,256,256]{2,1,0:T(8,128)S(1)}) custom-call(f32[1,2,256,256]{3,2,1,0:T(8,128)} %obj.1, f32[1,2,128,128]{3,2,1,0:T(8,128)} %probe.1, bf16[1,1,8,128,128]{4,3,2,1,0:T(8,128)(2,1)} %inten.1, bf16[4,256,256]{2,1,0:T(8,128)(2,1)} %constant.2.clone.tables, s32[1,8]{1,0:T(1,128)} %rows_in.1, s32[1,8]{1,0:T(1,128)} %cols_in.1, ...), custom_call_target="tpu_custom_call" | custom-call | tf_op jit(solution)/shard_map/refine/pallas_call | solution.py:496
  30.9 1.1 %put_out.1 = (f32[3,256,256]{2,1,0:T(8,128)}, f32[1,2,256,256]{3,2,1,0:T(8,128)}) custom-call(f32[3,256,256]{2,1,0:T(8,128)S(1)} %get-tuple-element.4.maps, f32[2,256,256]{2,1,0:T(8,128)S(1)} %get-tuple-element.5.model), custom_call_target="tpu_custom_call" | custom-call | tf_op jit(solution)/shard_map/put_out/pallas_call | solution.py:527
